TPU v7x, 512 devices: a whole 4x8x8 slice. The times are simulated.
512 devices in a mesh: layer: 16 (over z, core), col: 32 (over x, y).
Axes of the slice: x: 4, y: 8, z: 8, core: 2. Of those that a mesh axis runs over, the one named last changes fastest.
Arguments:
- factors: bfloat16 [16, 32, 2048, 64], P('layer', 'col'), may hold values from -0.9 to 0.9
- cores: float32 [16, 64, 64], P('layer'), may hold values from -2 to 6, as said below
- tile_list: int32 [256, 2], P('col'), may hold values from 0 to 31, as said below
- probes: bfloat16 [2048, 256, 64], P(None, 'col'), may hold values from -6 to 6
Outputs:
- basis: float32 [2048, 256, 64], P('layer', 'col')
- update_right: float32 [2048, 256, 64], P('layer', 'col')
Inputs may be any that keep to these rules, and one draw needn't show every extreme that they name: `tile_list`: each row is a block row and a block column of a tile of the lower triangle: the first is not below the second. `cores`: each matrix is symmetric positive definite: a Gram matrix plus a positive diagonal.
All inputs are finite; a program needn't handle non-finite values.
Results may differ from a plain program's by a relative error of at most 0.02.
Values may be sent and summed in bfloat16 or wider, within the bound.
No kernel may reach another device: no remote copies, remote signals or barrier semaphores. Data moves between devices by JAX's collectives and lax.ppermute only.
A program may use at most 64 MiB of HBM per device.

v0:
```python
import math

import jax
import jax.numpy as jnp
from jax import lax
from jax.experimental import pallas as pl
from jax.experimental.pallas import tpu as pltpu
from jax.sharding import Mesh, PartitionSpec as P


F32 = jnp.float32
BF16 = jnp.bfloat16
HIGHEST = lax.Precision.HIGHEST

NZ = 8
NT = 8
RANK = 64
PANELS = 8
DEPTH = PANELS * RANK
ROWS = 256
HALF = 128
BUNDLES = 24
EXTRA = 16


def nt_dot(a, b, precision=None):
    return lax.dot_general(
        a, b, (((1,), (1,)), ((), ())), precision=precision, preferred_element_type=F32
    )


def nn_dot(a, b, precision=None):
    return lax.dot_general(
        a, b, (((1,), (0,)), ((), ())), precision=precision, preferred_element_type=F32
    )


def split3(x):
    hi = x.astype(BF16)
    rest = x - hi.astype(F32)
    mid = rest.astype(BF16)
    low = (rest - mid.astype(F32)).astype(BF16)
    return hi, mid, low


def slice_kernel(f_ref, cores_ref, o_ref, sem):
    copies = []
    for q in range(NZ):
        copies.append(
            pltpu.make_async_copy(
                f_ref.at[:, q * ROWS:(q + 1) * ROWS], o_ref.at[q, :, 0:ROWS], sem.at[q]
            )
        )
        copies[q].start()
    one, two, _ = split3(cores_ref[...])
    both = jnp.concatenate([one, two], axis=1)
    for q in range(NZ):
        o_ref[q, :, ROWS:ROWS + 2 * RANK] = both
    for copy in copies:
        copy.wait()


def in_hbm(x):
    return pltpu.with_memory_space_constraint(x, pltpu.HBM)


def spread(own):
    def send(value, x_step, y_step):
        pairs = []
        for x in range(4):
            for y in range(8):
                if x_step is not None:
                    pairs.append((x * 8 + y, (x + x_step) % 4 * 8 + y))
                pairs.append((32 + x * 8 + y, 32 + x * 8 + (y + y_step) % 8))
        return lax.ppermute(value, ("core", "x", "y"), pairs)

    def bundle_send(value, y_step, x_step):
        pairs = []
        for x in range(4):
            for y in range(8):
                if y_step is not None:
                    pairs.append((x * 8 + y, x * 8 + (y + y_step) % 8))
                if x_step is not None:
                    pairs.append((32 + x * 8 + y, 32 + (x + x_step) % 4 * 8 + y))
        return lax.ppermute(value, ("core", "x", "y"), pairs)

    up1 = send(own, 1, 1)
    down1 = send(own, -1, -1)
    up2 = send(up1, 1, 1)
    down2 = send(down1, None, -1)
    up3 = send(up2, None, 1)
    down3 = send(down2, None, -1)
    up4 = send(up3, None, 1)
    near = [jnp.stack([own, up1]), jnp.stack([down1, up2])]
    far = [jnp.stack([down2, up3]), jnp.stack([down3, up4])]
    out1, out2, out3, a4, b4, a5, b5, a6, b6 = ([None, None] for _ in range(9))
    for h in range(2):
        out1[h] = bundle_send(near[h], 1, 1)
        out2[h] = bundle_send(near[h], -1, -1)
        out3[h] = bundle_send(out1[h], 1, 1)
        a4[h] = bundle_send(out2[h], -1, None)
        b4[h] = bundle_send(far[h], None, -1)
        a5[h] = bundle_send(out3[h], 1, None)
        b5[h] = bundle_send(far[h], None, 1)
        a6[h] = bundle_send(a4[h], -1, None)
        b6[h] = bundle_send(b4[h], None, -1)
    out7 = bundle_send(a5[0], 1, None)
    out8 = bundle_send(a6[1], -1, None)
    return (*near, *far, *out1, *out2, *out3, *a4, *b4, *a5, *b5, *a6, *b6, out7, out8)


def pick(index, *values):
    out = jnp.full_like(index, values[0])
    for number, value in enumerate(values[1:], 1):
        out = jnp.where(index == number, value, out)
    return out


def locate(rows):
    dx = (lax.axis_index("x").astype(jnp.int32) - rows // 8) % 4
    dy = (lax.axis_index("y").astype(jnp.int32) - rows % 8) % 8
    lower = lax.axis_index("core") == 0
    place0 = pick(dx, 0, 1, 3, 2)
    half0 = place0 // 2
    which0 = pick(dy, 0, 4, 8, 14, 22, 18, 10, 6) + half0
    place1 = pick(dy, 0, 1, 3, 1, 3, 2, 0, 2)
    half1 = place1 // 2
    which1 = jnp.where((dy <= 2) | (dy == 7), pick(dx, 0, 4, 8, 6), pick(dx, 2, 16, 20, 12)) + half1
    return jnp.where(lower, which0, which1), jnp.where(lower, place0 - 2 * half0, place1 - 2 * half1)


def sketch_kernel(first_ref, second_ref, z_ref, probe_ref, *refs):
    bundles, refs = refs[0:BUNDLES], refs[BUNDLES:]
    o_ref, left_ref, right_ref, slot_ref, sem_right, sem_left, sem_probe = refs
    start = pl.multiple_of(z_ref[0] * ROWS, ROWS)

    def fetch(place_ref, t, out_ref, sem):
        which, at = place_ref[0, t], place_ref[1, t]

        def choose(low, high):
            if high - low == 1:
                pltpu.make_async_copy(bundles[low].at[at], out_ref.at[t], sem.at[t]).start()
                return
            middle = (low + high) // 2

            @pl.when(which < middle)
            def _():
                choose(low, middle)

            @pl.when(which >= middle)
            def _():
                choose(middle, high)

        choose(0, BUNDLES)

    def arrived(t, out_ref, sem):
        pltpu.make_async_copy(bundles[0].at[0], out_ref.at[t], sem.at[t]).wait()

    probes = []
    for t in range(NT):
        probes.append(
            pltpu.make_async_copy(probe_ref.at[t, :, pl.ds(start, ROWS)], slot_ref.at[t], sem_probe.at[t])
        )
        probes[t].start()
        fetch(second_ref, t, right_ref, sem_right)
    for t in range(NT):
        fetch(first_ref, t, left_ref, sem_left)
    for t in range(NT):
        probes[t].wait()
        arrived(t, right_ref, sem_right)
        o_ref[t] = nt_dot(slot_ref[t], right_ref[t]).astype(BF16)
    for t in range(NT):
        arrived(t, left_ref, sem_left)


def core_products(total, cores_ref):
    parts = []
    for k in range(PANELS):
        block = total[:, k * RANK:(k + 1) * RANK]
        parts.append(nt_dot(block, cores_ref[k], HIGHEST))
    return parts


def first_kernel(part_ref, cores_ref, o_ref):
    total = part_ref[0].astype(F32)
    for q in range(1, NZ):
        total = total + part_ref[q].astype(F32)
    parts = core_products(total, cores_ref)
    for k in range(PANELS):
        half = parts[k].astype(BF16)
        for q in range(NZ):
            o_ref[q, :, k * RANK:(k + 1) * RANK] = half


def sample_kernel(core_ref, f_ref, o_ref):
    for t in range(NT):
        o_ref[t] = nn_dot(core_ref[t], f_ref[t]).astype(BF16)


def pack_gram(gram):
    row = lax.broadcasted_iota(jnp.int32, (RANK, RANK), 0)
    col = lax.broadcasted_iota(jnp.int32, (RANK, RANK), 1)
    one, two, three = (part.astype(F32) for part in split3(gram))
    diag = jnp.sum(jnp.where(row == col, two, 0.0), axis=1, keepdims=True)
    last = jnp.sum(jnp.where((row == RANK - 1) & (col == RANK - 1), two, 0.0), axis=(0, 1), keepdims=True)
    upper = jnp.where(col == row + 1, diag, 0.0)
    upper = jnp.where((row == 0) & (col == RANK - 1), last, upper)
    return jnp.where(col <= row, one, jnp.transpose(two)), jnp.where(col <= row, three, upper)


def unpack_gram(left, right):
    row = lax.broadcasted_iota(jnp.int32, (RANK, RANK), 0)
    col = lax.broadcasted_iota(jnp.int32, (RANK, RANK), 1)
    corner = (row == 0) & (col == RANK - 1)
    last = jnp.sum(jnp.where(corner, right, 0.0), axis=(0, 1), keepdims=True)
    diag = jnp.sum(jnp.where(col == row + 1, right, 0.0), axis=1, keepdims=True)
    two_diag = jnp.where((row == col) & (row < RANK - 1), diag, 0.0)
    two_diag = jnp.where((row == RANK - 1) & (col == RANK - 1), last, two_diag)
    lower = col <= row
    one = jnp.where(lower, left, 0.0)
    three = jnp.where(lower, right, 0.0)
    two = jnp.where(col > row, left, 0.0)
    strict = jnp.where(col < row, one, 0.0) + jnp.where(col < row, three, 0.0)
    full_diag = jnp.where(row == col, one + (three + two_diag), 0.0)
    below = strict + jnp.where(col < row, jnp.transpose(two), 0.0)
    return below + full_diag + jnp.transpose(below)


def fold(x):
    return jnp.concatenate([x[EXTRA * b:EXTRA * (b + 1)] for b in range(4)], axis=1)


def unfold(x):
    return jnp.concatenate([x[:, 128 * b:128 * (b + 1)] for b in range(4)], axis=0)


def gram_kernel(own_ref, other_ref, f_ref, o_ref):
    for t in range(NT):
        total = own_ref[t].astype(F32) + other_ref[t].astype(F32)
        gram = nt_dot(total, total, HIGHEST)
        hi = total.astype(BF16)
        low = (total - hi.astype(F32)).astype(BF16)
        both = nt_dot(jnp.concatenate([hi, low], axis=0), f_ref[t])
        o_ref[t, 0:RANK] = (both[0:RANK] + both[RANK:2 * RANK]).astype(BF16)
        left, right = pack_gram(gram)
        o_ref[t, RANK:RANK + EXTRA] = fold(jnp.concatenate([left, right], axis=1).astype(BF16))


def inverse_factor(gram):
    row_id = lax.broadcasted_iota(jnp.int32, (RANK, RANK), 0)
    col_id = lax.broadcasted_iota(jnp.int32, (RANK, RANK), 1)
    unit = jnp.where(row_id == col_id, 1.0, 0.0).astype(F32)
    work = jnp.concatenate([gram, unit], axis=1)
    blocks = [work[8 * b:8 * b + 8, :] for b in range(RANK // 8)]
    sub = lax.broadcasted_iota(jnp.int32, (8, 2 * RANK), 0)
    for p in range(RANK):
        home, at = divmod(p, 8)
        row = blocks[home][at:at + 1, :]
        pivot = row[:, p:p + 1]
        scaled = row * (1.0 / pivot)
        for b in range(home, RANK // 8):
            col = jnp.broadcast_to(blocks[b][:, p:p + 1], (8, 2 * RANK))
            if b == home:
                col = jnp.where(sub > at, col, 0.0)
            blocks[b] = blocks[b] - col * scaled
    work = jnp.concatenate(blocks, axis=0)
    diag = jnp.sum(jnp.where(row_id == col_id, work[:, 0:RANK], 0.0), axis=1, keepdims=True)
    return work[:, RANK:2 * RANK] * (1.0 / jnp.sqrt(diag))


def second_kernel(part_ref, cores_ref, o_ref):
    summed = part_ref[0].astype(F32)
    for q in range(1, NZ):
        summed = summed + part_ref[q].astype(F32)
    total = summed[0:RANK]
    packed = unfold(summed[RANK:RANK + EXTRA])
    gram = unpack_gram(packed[:, 0:RANK], packed[:, RANK:2 * RANK])
    inverse = inverse_factor(gram)
    projected = nn_dot(inverse, total, HIGHEST)
    parts = core_products(projected, cores_ref)
    one, two, _ = split3(inverse)
    extra = fold(jnp.concatenate([one, two], axis=1))
    for q in range(NZ):
        for k in range(PANELS):
            o_ref[q, 0:RANK, k * RANK:(k + 1) * RANK] = parts[k].astype(BF16)
        o_ref[q, RANK:RANK + EXTRA] = extra


def final_kernel(side_ref, core_ref, own_ref, other_ref, f_ref, basis_ref, keep_ref, send_ref):
    upper = side_ref[0] == 1
    for t in range(NT):
        extra = unfold(core_ref[t, RANK:RANK + EXTRA]).astype(F32)
        inverse = extra[:, 0:RANK] + extra[:, RANK:2 * RANK]
        total = own_ref[t].astype(F32) + other_ref[t].astype(F32)
        half = jnp.where(upper, total[:, HALF:ROWS], total[:, 0:HALF])
        basis_ref[t] = nn_dot(inverse, half, HIGHEST) * math.sqrt(2048.0)
        part = nn_dot(core_ref[t, 0:RANK], f_ref[t])
        first, last = part[:, 0:HALF], part[:, HALF:ROWS]
        keep_ref[t] = jnp.where(upper, last, first)
        send_ref[t] = jnp.where(upper, first, last).astype(BF16)


def local(factors, cores, tile_list, probes):
    swap = [(0, 1), (1, 0)]
    z = lax.axis_index("z").astype(jnp.int32).reshape(1)
    side = lax.axis_index("core").astype(jnp.int32).reshape(1)
    row_first = tile_list[:, 0].astype(jnp.int32)
    row_second = tile_list[:, 1].astype(jnp.int32)
    params = pltpu.CompilerParams(vmem_limit_bytes=32 * 1024 * 1024)

    smem = pl.BlockSpec(memory_space=pltpu.SMEM)
    hbm = pl.BlockSpec(memory_space=pl.ANY)
    vmem = pl.BlockSpec(memory_space=pltpu.VMEM)

    def call(kernel, out_shape, in_specs, *args, scratch=()):
        return pl.pallas_call(
            kernel,
            out_shape=out_shape,
            in_specs=in_specs,
            out_specs=jax.tree.map(lambda _: vmem, out_shape),
            scratch_shapes=scratch,
            compiler_params=params,
        )(*args)

    def shape(*dims, dtype=BF16):
        return jax.ShapeDtypeStruct(dims, dtype)

    def exchange(x):
        return lax.all_to_all(x, "z", 0, 0, tiled=True)

    mine = jnp.transpose(factors[0, 0], (1, 0))
    sliced = call(
        slice_kernel,
        shape(NZ, RANK, ROWS + 2 * RANK),
        [hbm, vmem],
        in_hbm(mine),
        cores[0],
        scratch=[pltpu.SemaphoreType.DMA((NZ,))],
    )
    panels = exchange(sliced)
    pieces = panels[:, :, ROWS:ROWS + 2 * RANK].astype(F32)
    all_cores = pieces[:, :, 0:RANK] + pieces[:, :, RANK:2 * RANK]
    bundles = spread(panels[:, :, 0:ROWS].reshape(DEPTH, ROWS))
    probe = in_hbm(jnp.transpose(probes, (1, 2, 0)))
    block = shape(NT, DEPTH, ROWS)
    sketch, left, right = call(
        sketch_kernel,
        (shape(NT, RANK, DEPTH), block, block),
        [smem, smem, smem] + [hbm] * (1 + BUNDLES),
        jnp.stack(locate(row_first)),
        jnp.stack(locate(row_second)),
        z,
        probe,
        *(in_hbm(bundle) for bundle in bundles),
        scratch=[pltpu.VMEM((NT, RANK, ROWS), BF16)] + [pltpu.SemaphoreType.DMA((NT,))] * 3,
    )
    first = call(first_kernel, shape(NZ, RANK, DEPTH), [vmem] * 2, exchange(sketch), all_cores)
    own = call(sample_kernel, shape(NT, RANK, ROWS), [vmem] * 2, exchange(first), left)
    other = lax.ppermute(own, "core", swap)
    tall = (NT, RANK + EXTRA, DEPTH)
    stacked = call(gram_kernel, shape(*tall), [vmem] * 3, own, other, left)
    second = call(second_kernel, shape(*tall), [vmem] * 2, exchange(stacked), all_cores)
    half = (NT, RANK, HALF)
    basis, keep, send = call(
        final_kernel,
        (shape(*half, dtype=F32), shape(*half, dtype=F32), shape(*half)),
        [smem] + [vmem] * 4,
        side,
        exchange(second),
        own,
        other,
        right,
    )
    update = keep + lax.ppermute(send, "core", swap).astype(F32)
    return jnp.transpose(basis, (2, 0, 1)), jnp.transpose(update, (2, 0, 1))


def solution(mesh):
    fine = Mesh(mesh.devices.reshape(8, 2, 4, 8), ("z", "core", "x", "y"))
    layer, col = ("z", "core"), ("x", "y")
    placed = (
        P(layer, col, None, None),
        P(layer, None, None),
        P(col, None),
        P(None, col, None),
    )
    return jax.shard_map(
        local,
        mesh=fine,
        in_specs=placed,
        out_specs=(P(layer, col, None), P(layer, col, None)),
        check_vma=False,
    )
```

profile of v0, /device:TPU:1, one launch (start us, length us, event | category | flops | bytes accessed | tf_op | source)
XLA Modules:
  0.0 217.9 jit_solution(9422928392488131784)
XLA Ops:
  2.3 24.2 %all_to_all.25 = bf16[8,64,384]{2,1,0:T(8,128)(2,1)S(1)} all-to-all(bf16[8,64,384]{2,1,0:T(8,128)(2,1)S(1)} %shard_map.59), channel_id=1, replica_groups=mesh['z'=8,'core'=2,'x'=4,'y'=8] {'z'}, dimensions={0} | all-to-all | bytes 786432 | tf_op jit(solution)/shard_map/all_to_all | solution.py:329
  26.6 3.2 %collective-permute-start = (bf16[512,256]{1,0:T(8,128)(2,1)S(1)}, bf16[512,256]{1,0:T(8,128)(2,1)S(1)}, u32[]{:S(2)}, u32[]{:S(2)}) collective-permute-start(bf16[512,256]{1,0:T(8,128)(2,1)S(1)} %bitcast.57), channel_id=1, source_target_pairs={{0,8},{32,33},{1,9},{33,34},{2,10},{34,35},{3,11},{35,36},{4,12},{... | collective-permute-start | bytes 786440 | tf_op jit(solution)/shard_map/ppermute | solution.py:75
  29.8 3.8 %collective-permute-start.1 = (bf16[512,256]{1,0:T(8,128)(2,1)S(1)}, bf16[512,256]{1,0:T(8,128)(2,1)S(1)}, u32[]{:S(2)}, u32[]{:S(2)}) collective-permute-start(bf16[512,256]{1,0:T(8,128)(2,1)S(1)} %bitcast.58), channel_id=1, source_target_pairs={{0,24},{32,39},{1,25},{33,32},{2,26},{34,33},{3,27},{35,34},{4,28}... | collective-permute-start | bytes 786440 | tf_op jit(solution)/shard_map/ppermute | solution.py:75
  33.6 2.1 collective-permute-done
  35.7 1.9 collective-permute-start.2
  37.7 4.6 %collective-permute-start.3 = (bf16[512,256]{1,0:T(8,128)(2,1)S(1)}, bf16[512,256]{1,0:T(8,128)(2,1)S(1)}, u32[]{:S(2)}, u32[]{:S(2)}) collective-permute-start(bf16[512,256]{1,0:T(8,128)(2,1)S(1)} %collective-permute-done.1), channel_id=1, source_target_pairs={{32,39},{33,32},{34,33},{35,34},{36,35},{37,36},{38,37},{39,38},{4... | collective-permute-start | bytes 786440 | tf_op jit(solution)/shard_map/ppermute | solution.py:75
  42.2 1.8 collective-permute-done.2
  44.1 1.9 collective-permute-start.4
  46.0 4.9 %collective-permute-start.5 = (bf16[512,256]{1,0:T(8,128)(2,1)S(1)}, bf16[512,256]{1,0:T(8,128)(2,1)S(1)}, u32[]{:S(2)}, u32[]{:S(2)}) collective-permute-start(bf16[512,256]{1,0:T(8,128)(2,1)S(1)} %collective-permute-done.3), channel_id=1, source_target_pairs={{32,39},{33,32},{34,33},{35,34},{36,35},{37,36},{38,37},{39,38},{4... | collective-permute-start | bytes 786440 | tf_op jit(solution)/shard_map/ppermute | solution.py:75
  50.9 1.5 collective-permute-done.4
  52.4 1.9 collective-permute-start.6
  54.4 4.1 %collective-permute-start.9 = (bf16[2,512,256]{2,1,0:T(8,128)(2,1)S(1)}, bf16[2,512,256]{2,1,0:T(8,128)(2,1)S(1)}, u32[]{:S(2)}, u32[]{:S(2)}) collective-permute-start(bf16[2,512,256]{2,1,0:T(8,128)(2,1)S(1)} %pad_maximum_fusion.refs_0_), channel_id=1, source_target_pairs={{0,7},{32,56},{1,0},{33,57},{2,1},{34,58},{3,2},{35,59},{4,3},{36,... | collective-permute-start | bytes 1572872 | tf_op jit(solution)/shard_map/ppermute | solution.py:85
  58.5 1.9 collective-permute-start.7
  60.5 4.6 %collective-permute-start.10 = (bf16[2,512,256]{2,1,0:T(8,128)(2,1)S(1)}, bf16[2,512,256]{2,1,0:T(8,128)(2,1)S(1)}, u32[]{:S(2)}, u32[]{:S(2)}) collective-permute-start(bf16[2,512,256]{2,1,0:T(8,128)(2,1)S(1)} %pad_maximum_fusion.1.refs_1_), channel_id=1, source_target_pairs={{0,7},{32,56},{1,0},{33,57},{2,1},{34,58},{3,2},{35,59},{4,3},{36,... | collective-permute-start | bytes 1572872 | tf_op jit(solution)/shard_map/ppermute | solution.py:85
  65.1 1.9 collective-permute-start.8
  67.1 1.9 collective-permute-start.19
  69.1 4.6 %collective-permute-start.15 = (bf16[2,512,256]{2,1,0:T(8,128)(2,1)S(1)}, bf16[2,512,256]{2,1,0:T(8,128)(2,1)}, u32[]{:S(2)}, u32[]{:S(2)}) collective-permute-start(bf16[2,512,256]{2,1,0:T(8,128)(2,1)S(1)} %pad_maximum_fusion.2.refs_2_), channel_id=1, source_target_pairs={{32,56},{33,57},{34,58},{35,59},{36,60},{37,61},{38,62},{39,63},{4... | collective-permute-start | bytes 1572872 | tf_op jit(solution)/shard_map/ppermute | solution.py:85
  73.7 1.5 collective-permute-start.13
  75.2 1.9 collective-permute-start.11
  77.1 2.8 %collective-permute-start.20 = (bf16[2,512,256]{2,1,0:T(8,128)(2,1)S(1)}, bf16[2,512,256]{2,1,0:T(8,128)(2,1)S(1)}, u32[]{:S(2)}, u32[]{:S(2)}) collective-permute-start(bf16[2,512,256]{2,1,0:T(8,128)(2,1)S(1)} %pad_maximum_fusion.3.refs_3_), channel_id=1, source_target_pairs={{32,40},{33,41},{34,42},{35,43},{36,44},{37,45},{38,46},{39,47},{4... | collective-permute-start | bytes 1572872 | tf_op jit(solution)/shard_map/ppermute | solution.py:85
  79.9 2.4 %collective-permute-done.19.refs_16_ = bf16[2,512,256]{2,1,0:T(8,128)(2,1)S(1)} collective-permute-done((bf16[2,512,256]{2,1,0:T(8,128)(2,1)S(1)}, bf16[2,512,256]{2,1,0:T(8,128)(2,1)S(1)}, u32[]{:S(2)}, u32[]{:S(2)}) %collective-permute-start.19) | collective-permute-done | bytes 524320 | tf_op jit(solution)/shard_map/ppermute | solution.py:85
  82.3 1.5 collective-permute-start.14
  83.8 1.9 collective-permute-start.16
  85.7 3.4 %collective-permute-start.12 = (bf16[2,512,256]{2,1,0:T(8,128)(2,1)}, bf16[2,512,256]{2,1,0:T(8,128)(2,1)}, u32[]{:S(2)}, u32[]{:S(2)}) collective-permute-start(bf16[2,512,256]{2,1,0:T(8,128)(2,1)} %collective-permute-done.8.refs_5_), channel_id=1, source_target_pairs={{0,1},{32,40},{1,2},{33,41},{2,3},{34,42},{3,4},{35,43},{4,5},{36,... | collective-permute-start | bytes 1572872 | tf_op jit(solution)/shard_map/ppermute | solution.py:85
  89.1 3.1 %collective-permute-start.23 = (bf16[2,512,256]{2,1,0:T(8,128)(2,1)}, bf16[2,512,256]{2,1,0:T(8,128)(2,1)}, u32[]{:S(2)}, u32[]{:S(2)}) collective-permute-start(bf16[2,512,256]{2,1,0:T(8,128)(2,1)} %collective-permute-done.15.refs_12_), channel_id=1, source_target_pairs={{32,56},{33,57},{34,58},{35,59},{36,60},{37,61},{38,62},{39,63},{4... | collective-permute-start | bytes 1572872 | tf_op jit(solution)/shard_map/ppermute | solution.py:85
  92.2 1.3 collective-permute-done.20.refs_17_
  93.5 1.5 collective-permute-start.17
  95.0 1.5 collective-permute-start.22
  97.0 1.5 collective-permute-start.21
  98.8 1.9 collective-permute-start.24
  100.8 1.5 collective-permute-start.18
  102.3 1.5 collective-permute-start.25
  103.7 1.5 collective-permute-start.26
  107.8 1.6 collective-permute-done.24.refs_21_
  109.4 4.3 %shard_map.60 = (bf16[8,64,512]{2,1,0:T(8,128)(2,1)}, bf16[8,512,256]{2,1,0:T(8,128)(2,1)S(1)}, bf16[8,512,256]{2,1,0:T(8,128)(2,1)S(1)}) custom-call(s32[2,8]{1,0:T(2,128)S(1)} %pad_add_fusion.first_ref, s32[2,8]{1,0:T(2,128)S(1)} %pad_add_fusion.1.second_ref, s32[1]{0:T(128)} %bitcast.3.z_ref, bf16[8,64,2048]{2,1,0:T(8,128)(2,1)} %bitcast.56, ...), custom_call_target="tpu_custom_call" | custom-call | tf_op jit(solution)/shard_map/pallas_call | solution.py:316
  113.8 1.3 copy-done
  115.1 3.5 %all-to-all-start.1 = ((bf16[8,64,512]{2,1,0:T(8,128)(2,1)}), bf16[8,64,512]{2,1,0:T(8,128)(2,1)S(1)}, u32[]{:S(2)}, u32[]{:S(2)}) async-start(bf16[8,64,512]{2,1,0:T(8,128)(2,1)} %get-tuple-element.8), calls=%async_computation.1 | async-start | bytes 1048576 | tf_op jit(solution)/shard_map/all_to_all | solution.py:329
  118.7 12.0 %all-to-all-done.1.part_ref = bf16[8,64,512]{2,1,0:T(8,128)(2,1)S(1)} async-done(((bf16[8,64,512]{2,1,0:T(8,128)(2,1)}), bf16[8,64,512]{2,1,0:T(8,128)(2,1)S(1)}, u32[]{:S(2)}, u32[]{:S(2)}) %all-to-all-start.1) | async-done | bytes 524320 | tf_op jit(solution)/shard_map/all_to_all | solution.py:329
  131.4 14.7 %all_to_all.26.core_ref = bf16[8,64,512]{2,1,0:T(8,128)(2,1)S(1)} all-to-all(bf16[8,64,512]{2,1,0:T(8,128)(2,1)S(1)} %shard_map.61), channel_id=1, replica_groups=mesh['z'=8,'core'=2,'x'=4,'y'=8] {'z'}, dimensions={0} | all-to-all | bytes 1048576 | tf_op jit(solution)/shard_map/all_to_all | solution.py:329
  146.6 10.3 %collective-permute-start.27 = (bf16[8,64,256]{2,1,0:T(8,128)(2,1)S(1)}, bf16[8,64,256]{2,1,0:T(8,128)(2,1)S(1)}, u32[]{:S(2)}, u32[]{:S(2)}) collective-permute-start(bf16[8,64,256]{2,1,0:T(8,128)(2,1)S(1)} %shard_map.62.own_ref), channel_id=1, source_target_pairs={{0,32},{32,0},{1,33},{33,1},{2,34},{34,2},{3,35},{35,3},{4,36},{36... | collective-permute-start | bytes 786440 | tf_op jit(solution)/shard_map/ppermute | solution.py:359
  156.9 1.1 collective-permute-done.27.other_ref
  158.0 1.4 shard_map.63
  159.4 23.3 %all_to_all.27.part_ref = bf16[8,80,512]{2,1,0:T(8,128)(2,1)S(1)} all-to-all(bf16[8,80,512]{2,1,0:T(8,128)(2,1)S(1)} %shard_map.63), channel_id=1, replica_groups=mesh['z'=8,'core'=2,'x'=4,'y'=8] {'z'}, dimensions={0} | all-to-all | bytes 1310720 | tf_op jit(solution)/shard_map/all_to_all | solution.py:329
  182.7 6.6 %shard_map.64 = bf16[8,80,512]{2,1,0:T(8,128)(2,1)S(1)} custom-call(bf16[8,80,512]{2,1,0:T(8,128)(2,1)S(1)} %all_to_all.27.part_ref, f32[8,64,64]{2,1,0:T(8,128)S(1)} %slice_add_fusion.cores_ref), custom_call_target="tpu_custom_call" | custom-call | tf_op jit(solution)/shard_map/pallas_call | solution.py:316
  189.3 22.3 %all_to_all.28.core_ref = bf16[8,80,512]{2,1,0:T(8,128)(2,1)S(1)} all-to-all(bf16[8,80,512]{2,1,0:T(8,128)(2,1)S(1)} %shard_map.64), channel_id=1, replica_groups=mesh['z'=8,'core'=2,'x'=4,'y'=8] {'z'}, dimensions={0} | all-to-all | bytes 1310720 | tf_op jit(solution)/shard_map/all_to_all | solution.py:329
  211.6 1.4 shard_map.65
  213.0 3.3 %collective-permute-start.28 = (bf16[8,64,128]{2,1,0:T(8,128)(2,1)S(1)}, bf16[8,64,128]{2,1,0:T(8,128)(2,1)S(1)}, u32[]{:S(2)}, u32[]{:S(2)}) collective-permute-start(bf16[8,64,128]{2,1,0:T(8,128)(2,1)S(1)} %get-tuple-element.13), channel_id=1, source_target_pairs={{0,32},{32,0},{1,33},{33,1},{2,34},{34,2},{3,35},{35,3},{4,36},{36... | collective-permute-start | bytes 393224 | tf_op jit(solution)/shard_map/ppermute | solution.py:374
  216.2 1.0 collective-permute-done.28
  (62 shorter events, 7.4 us)
Async XLA Ops:
  0.6 0.8 copy-start.2
  26.6 9.1 %collective-permute-start = (bf16[512,256]{1,0:T(8,128)(2,1)S(1)}, bf16[512,256]{1,0:T(8,128)(2,1)S(1)}, u32[]{:S(2)}, u32[]{:S(2)}) collective-permute-start(bf16[512,256]{1,0:T(8,128)(2,1)S(1)} %bitcast.57), channel_id=1, source_target_pairs={{0,8},{32,33},{1,9},{33,34},{2,10},{34,35},{3,11},{35,36},{4,12},{... | collective-permute-start | bytes 786440 | tf_op jit(solution)/shard_map/ppermute | solution.py:75
  29.8 7.9 %collective-permute-start.1 = (bf16[512,256]{1,0:T(8,128)(2,1)S(1)}, bf16[512,256]{1,0:T(8,128)(2,1)S(1)}, u32[]{:S(2)}, u32[]{:S(2)}) collective-permute-start(bf16[512,256]{1,0:T(8,128)(2,1)S(1)} %bitcast.58), channel_id=1, source_target_pairs={{0,24},{32,39},{1,25},{33,32},{2,26},{34,33},{3,27},{35,34},{4,28}... | collective-permute-start | bytes 786440 | tf_op jit(solution)/shard_map/ppermute | solution.py:75
  35.7 8.3 %collective-permute-start.2 = (bf16[512,256]{1,0:T(8,128)(2,1)S(1)}, bf16[512,256]{1,0:T(8,128)(2,1)S(1)}, u32[]{:S(2)}, u32[]{:S(2)}) collective-permute-start(bf16[512,256]{1,0:T(8,128)(2,1)S(1)} %collective-permute-done), channel_id=1, source_target_pairs={{0,8},{32,33},{1,9},{33,34},{2,10},{34,35},{3,11},{35,36},{4,12},{... | collective-permute-start | bytes 786440 | tf_op jit(solution)/shard_map/ppermute | solution.py:75
  37.7 8.3 %collective-permute-start.3 = (bf16[512,256]{1,0:T(8,128)(2,1)S(1)}, bf16[512,256]{1,0:T(8,128)(2,1)S(1)}, u32[]{:S(2)}, u32[]{:S(2)}) collective-permute-start(bf16[512,256]{1,0:T(8,128)(2,1)S(1)} %collective-permute-done.1), channel_id=1, source_target_pairs={{32,39},{33,32},{34,33},{35,34},{36,35},{37,36},{38,37},{39,38},{4... | collective-permute-start | bytes 786440 | tf_op jit(solution)/shard_map/ppermute | solution.py:75
  44.1 8.3 %collective-permute-start.4 = (bf16[512,256]{1,0:T(8,128)(2,1)S(1)}, bf16[512,256]{1,0:T(8,128)(2,1)S(1)}, u32[]{:S(2)}, u32[]{:S(2)}) collective-permute-start(bf16[512,256]{1,0:T(8,128)(2,1)S(1)} %collective-permute-done.2), channel_id=1, source_target_pairs={{32,33},{33,34},{34,35},{35,36},{36,37},{37,38},{38,39},{39,32},{4... | collective-permute-start | bytes 786440 | tf_op jit(solution)/shard_map/ppermute | solution.py:75
  46.0 19.1 %collective-permute-start.5 = (bf16[512,256]{1,0:T(8,128)(2,1)S(1)}, bf16[512,256]{1,0:T(8,128)(2,1)S(1)}, u32[]{:S(2)}, u32[]{:S(2)}) collective-permute-start(bf16[512,256]{1,0:T(8,128)(2,1)S(1)} %collective-permute-done.3), channel_id=1, source_target_pairs={{32,39},{33,32},{34,33},{35,34},{36,35},{37,36},{38,37},{39,38},{4... | collective-permute-start | bytes 786440 | tf_op jit(solution)/shard_map/ppermute | solution.py:75
  52.4 14.7 %collective-permute-start.6 = (bf16[512,256]{1,0:T(8,128)(2,1)S(1)}, bf16[512,256]{1,0:T(8,128)(2,1)S(1)}, u32[]{:S(2)}, u32[]{:S(2)}) collective-permute-start(bf16[512,256]{1,0:T(8,128)(2,1)S(1)} %collective-permute-done.4), channel_id=1, source_target_pairs={{32,33},{33,34},{34,35},{35,36},{36,37},{37,38},{38,39},{39,32},{4... | collective-permute-start | bytes 786440 | tf_op jit(solution)/shard_map/ppermute | solution.py:75
  54.3 42.2 %copy-start.12 = (s32[8,2]{0,1:T(2,128)S(1)}, s32[8,2]{0,1:T(2,128)}, u32[]{:S(2)}) copy-start(s32[8,2]{0,1:T(2,128)} %param.6) | copy-start | bytes 196
  54.4 55.1 %copy-start.3 = (bf16[2,512,256]{2,1,0:T(8,128)(2,1)}, bf16[2,512,256]{2,1,0:T(8,128)(2,1)S(1)}, u32[]{:S(2)}) copy-start(bf16[2,512,256]{2,1,0:T(8,128)(2,1)S(1)} %pad_maximum_fusion.refs_0_) | copy-start | bytes 1572868
  54.4 14.7 %collective-permute-start.9 = (bf16[2,512,256]{2,1,0:T(8,128)(2,1)S(1)}, bf16[2,512,256]{2,1,0:T(8,128)(2,1)S(1)}, u32[]{:S(2)}, u32[]{:S(2)}) collective-permute-start(bf16[2,512,256]{2,1,0:T(8,128)(2,1)S(1)} %pad_maximum_fusion.refs_0_), channel_id=1, source_target_pairs={{0,7},{32,56},{1,0},{33,57},{2,1},{34,58},{3,2},{35,59},{4,3},{36,... | collective-permute-start | bytes 1572872 | tf_op jit(solution)/shard_map/ppermute | solution.py:85
  58.5 15.2 %collective-permute-start.7 = (bf16[2,512,256]{2,1,0:T(8,128)(2,1)S(1)}, bf16[2,512,256]{2,1,0:T(8,128)(2,1)S(1)}, u32[]{:S(2)}, u32[]{:S(2)}) collective-permute-start(bf16[2,512,256]{2,1,0:T(8,128)(2,1)S(1)} %pad_maximum_fusion.refs_0_), channel_id=1, source_target_pairs={{0,1},{32,40},{1,2},{33,41},{2,3},{34,42},{3,4},{35,43},{4,5},{36,... | collective-permute-start | bytes 1572872 | tf_op jit(solution)/shard_map/ppermute | solution.py:85
  60.5 49.0 %copy-start.4 = (bf16[2,512,256]{2,1,0:T(8,128)(2,1)}, bf16[2,512,256]{2,1,0:T(8,128)(2,1)S(1)}, u32[]{:S(2)}) copy-start(bf16[2,512,256]{2,1,0:T(8,128)(2,1)S(1)} %pad_maximum_fusion.1.refs_1_) | copy-start | bytes 1572868
  60.5 14.7 %collective-permute-start.10 = (bf16[2,512,256]{2,1,0:T(8,128)(2,1)S(1)}, bf16[2,512,256]{2,1,0:T(8,128)(2,1)S(1)}, u32[]{:S(2)}, u32[]{:S(2)}) collective-permute-start(bf16[2,512,256]{2,1,0:T(8,128)(2,1)S(1)} %pad_maximum_fusion.1.refs_1_), channel_id=1, source_target_pairs={{0,7},{32,56},{1,0},{33,57},{2,1},{34,58},{3,2},{35,59},{4,3},{36,... | collective-permute-start | bytes 1572872 | tf_op jit(solution)/shard_map/ppermute | solution.py:85
  65.1 12.0 %copy-start.5 = (bf16[2,512,256]{2,1,0:T(8,128)(2,1)}, bf16[2,512,256]{2,1,0:T(8,128)(2,1)S(1)}, u32[]{:S(2)}) copy-start(bf16[2,512,256]{2,1,0:T(8,128)(2,1)S(1)} %pad_maximum_fusion.2.refs_2_) | copy-start | bytes 1572868
  65.1 12.0 %collective-permute-start.8 = (bf16[2,512,256]{2,1,0:T(8,128)(2,1)S(1)}, bf16[2,512,256]{2,1,0:T(8,128)(2,1)}, u32[]{:S(2)}, u32[]{:S(2)}) collective-permute-start(bf16[2,512,256]{2,1,0:T(8,128)(2,1)S(1)} %pad_maximum_fusion.1.refs_1_), channel_id=1, source_target_pairs={{0,1},{32,40},{1,2},{33,41},{2,3},{34,42},{3,4},{35,43},{4,5},{36,... | collective-permute-start | bytes 1572872 | tf_op jit(solution)/shard_map/ppermute | solution.py:85
  67.1 15.2 %collective-permute-start.19 = (bf16[2,512,256]{2,1,0:T(8,128)(2,1)S(1)}, bf16[2,512,256]{2,1,0:T(8,128)(2,1)S(1)}, u32[]{:S(2)}, u32[]{:S(2)}) collective-permute-start(bf16[2,512,256]{2,1,0:T(8,128)(2,1)S(1)} %pad_maximum_fusion.2.refs_2_), channel_id=1, source_target_pairs={{32,40},{33,41},{34,42},{35,43},{36,44},{37,45},{38,46},{39,47},{4... | collective-permute-start | bytes 1572872 | tf_op jit(solution)/shard_map/ppermute | solution.py:85
  69.1 40.3 %copy-start.6 = (bf16[2,512,256]{2,1,0:T(8,128)(2,1)}, bf16[2,512,256]{2,1,0:T(8,128)(2,1)S(1)}, u32[]{:S(2)}) copy-start(bf16[2,512,256]{2,1,0:T(8,128)(2,1)S(1)} %pad_maximum_fusion.3.refs_3_) | copy-start | bytes 1572868
  69.1 40.3 %copy-start.7 = (bf16[2,512,256]{2,1,0:T(8,128)(2,1)}, bf16[2,512,256]{2,1,0:T(8,128)(2,1)S(1)}, u32[]{:S(2)}) copy-start(bf16[2,512,256]{2,1,0:T(8,128)(2,1)S(1)} %collective-permute-done.9.refs_6_) | copy-start | bytes 1572868
  69.1 14.7 %collective-permute-start.15 = (bf16[2,512,256]{2,1,0:T(8,128)(2,1)S(1)}, bf16[2,512,256]{2,1,0:T(8,128)(2,1)}, u32[]{:S(2)}, u32[]{:S(2)}) collective-permute-start(bf16[2,512,256]{2,1,0:T(8,128)(2,1)S(1)} %pad_maximum_fusion.2.refs_2_), channel_id=1, source_target_pairs={{32,56},{33,57},{34,58},{35,59},{36,60},{37,61},{38,62},{39,63},{4... | collective-permute-start | bytes 1572872 | tf_op jit(solution)/shard_map/ppermute | solution.py:85
  73.7 35.7 %copy-start.8 = (bf16[2,512,256]{2,1,0:T(8,128)(2,1)}, bf16[2,512,256]{2,1,0:T(8,128)(2,1)S(1)}, u32[]{:S(2)}) copy-start(bf16[2,512,256]{2,1,0:T(8,128)(2,1)S(1)} %collective-permute-done.7.refs_4_) | copy-start | bytes 1572868
  73.7 12.0 %collective-permute-start.13 = (bf16[2,512,256]{2,1,0:T(8,128)(2,1)S(1)}, bf16[2,512,256]{2,1,0:T(8,128)(2,1)}, u32[]{:S(2)}, u32[]{:S(2)}) collective-permute-start(bf16[2,512,256]{2,1,0:T(8,128)(2,1)S(1)} %collective-permute-done.9.refs_6_), channel_id=1, source_target_pairs={{0,7},{1,0},{2,1},{3,2},{4,3},{5,4},{6,5},{7,6},{8,15},{9,8},{10,9... | collective-permute-start | bytes 1572872 | tf_op jit(solution)/shard_map/ppermute | solution.py:85
  75.2 34.2 %copy-start.9 = (bf16[2,512,256]{2,1,0:T(8,128)(2,1)}, bf16[2,512,256]{2,1,0:T(8,128)(2,1)S(1)}, u32[]{:S(2)}) copy-start(bf16[2,512,256]{2,1,0:T(8,128)(2,1)S(1)} %collective-permute-done.10.refs_7_) | copy-start | bytes 1572868
  75.2 13.9 %collective-permute-start.11 = (bf16[2,512,256]{2,1,0:T(8,128)(2,1)S(1)}, bf16[2,512,256]{2,1,0:T(8,128)(2,1)}, u32[]{:S(2)}, u32[]{:S(2)}) collective-permute-start(bf16[2,512,256]{2,1,0:T(8,128)(2,1)S(1)} %collective-permute-done.7.refs_4_), channel_id=1, source_target_pairs={{0,1},{32,40},{1,2},{33,41},{2,3},{34,42},{3,4},{35,43},{4,5},{36,... | collective-permute-start | bytes 1572872 | tf_op jit(solution)/shard_map/ppermute | solution.py:85
  77.1 16.4 %collective-permute-start.20 = (bf16[2,512,256]{2,1,0:T(8,128)(2,1)S(1)}, bf16[2,512,256]{2,1,0:T(8,128)(2,1)S(1)}, u32[]{:S(2)}, u32[]{:S(2)}) collective-permute-start(bf16[2,512,256]{2,1,0:T(8,128)(2,1)S(1)} %pad_maximum_fusion.3.refs_3_), channel_id=1, source_target_pairs={{32,40},{33,41},{34,42},{35,43},{36,44},{37,45},{38,46},{39,47},{4... | collective-permute-start | bytes 1572872 | tf_op jit(solution)/shard_map/ppermute | solution.py:85
  82.3 12.8 %copy-start.10 = (bf16[2,512,256]{2,1,0:T(8,128)(2,1)}, bf16[2,512,256]{2,1,0:T(8,128)(2,1)S(1)}, u32[]{:S(2)}) copy-start(bf16[2,512,256]{2,1,0:T(8,128)(2,1)S(1)} %collective-permute-done.19.refs_16_) | copy-start | bytes 1572868
  82.3 12.7 %collective-permute-start.14 = (bf16[2,512,256]{2,1,0:T(8,128)(2,1)S(1)}, bf16[2,512,256]{2,1,0:T(8,128)(2,1)}, u32[]{:S(2)}, u32[]{:S(2)}) collective-permute-start(bf16[2,512,256]{2,1,0:T(8,128)(2,1)S(1)} %collective-permute-done.10.refs_7_), channel_id=1, source_target_pairs={{0,7},{1,0},{2,1},{3,2},{4,3},{5,4},{6,5},{7,6},{8,15},{9,8},{10,9... | collective-permute-start | bytes 1572872 | tf_op jit(solution)/shard_map/ppermute | solution.py:85
  83.8 13.3 %collective-permute-start.16 = (bf16[2,512,256]{2,1,0:T(8,128)(2,1)S(1)}, bf16[2,512,256]{2,1,0:T(8,128)(2,1)}, u32[]{:S(2)}, u32[]{:S(2)}) collective-permute-start(bf16[2,512,256]{2,1,0:T(8,128)(2,1)S(1)} %pad_maximum_fusion.3.refs_3_), channel_id=1, source_target_pairs={{32,56},{33,57},{34,58},{35,59},{36,60},{37,61},{38,62},{39,63},{4... | collective-permute-start | bytes 1572872 | tf_op jit(solution)/shard_map/ppermute | solution.py:85
  85.7 13.2 %collective-permute-start.12 = (bf16[2,512,256]{2,1,0:T(8,128)(2,1)}, bf16[2,512,256]{2,1,0:T(8,128)(2,1)}, u32[]{:S(2)}, u32[]{:S(2)}) collective-permute-start(bf16[2,512,256]{2,1,0:T(8,128)(2,1)} %collective-permute-done.8.refs_5_), channel_id=1, source_target_pairs={{0,1},{32,40},{1,2},{33,41},{2,3},{34,42},{3,4},{35,43},{4,5},{36,... | collective-permute-start | bytes 1572872 | tf_op jit(solution)/shard_map/ppermute | solution.py:85
  89.1 11.7 %collective-permute-start.23 = (bf16[2,512,256]{2,1,0:T(8,128)(2,1)}, bf16[2,512,256]{2,1,0:T(8,128)(2,1)}, u32[]{:S(2)}, u32[]{:S(2)}) collective-permute-start(bf16[2,512,256]{2,1,0:T(8,128)(2,1)} %collective-permute-done.15.refs_12_), channel_id=1, source_target_pairs={{32,56},{33,57},{34,58},{35,59},{36,60},{37,61},{38,62},{39,63},{4... | collective-permute-start | bytes 1572872 | tf_op jit(solution)/shard_map/ppermute | solution.py:85
  93.5 3.0 %copy-start.11 = (bf16[2,512,256]{2,1,0:T(8,128)(2,1)}, bf16[2,512,256]{2,1,0:T(8,128)(2,1)S(1)}, u32[]{:S(2)}) copy-start(bf16[2,512,256]{2,1,0:T(8,128)(2,1)S(1)} %collective-permute-done.20.refs_17_) | copy-start | bytes 1572868
  93.5 8.8 %collective-permute-start.17 = (bf16[2,512,256]{2,1,0:T(8,128)(2,1)}, bf16[2,512,256]{2,1,0:T(8,128)(2,1)}, u32[]{:S(2)}, u32[]{:S(2)}) collective-permute-start(bf16[2,512,256]{2,1,0:T(8,128)(2,1)} %collective-permute-done.11.refs_8_), channel_id=1, source_target_pairs={{0,1},{1,2},{2,3},{3,4},{4,5},{5,6},{6,7},{7,0},{8,9},{9,10},{10,1... | collective-permute-start | bytes 1572872 | tf_op jit(solution)/shard_map/ppermute | solution.py:85
  95.0 8.7 %collective-permute-start.22 = (bf16[2,512,256]{2,1,0:T(8,128)(2,1)}, bf16[2,512,256]{2,1,0:T(8,128)(2,1)}, u32[]{:S(2)}, u32[]{:S(2)}) collective-permute-start(bf16[2,512,256]{2,1,0:T(8,128)(2,1)} %collective-permute-done.14.refs_11_), channel_id=1, source_target_pairs={{0,7},{1,0},{2,1},{3,2},{4,3},{5,4},{6,5},{7,6},{8,15},{9,8},{10,9... | collective-permute-start | bytes 1572872 | tf_op jit(solution)/shard_map/ppermute | solution.py:85
  97.0 10.7 %collective-permute-start.21 = (bf16[2,512,256]{2,1,0:T(8,128)(2,1)}, bf16[2,512,256]{2,1,0:T(8,128)(2,1)}, u32[]{:S(2)}, u32[]{:S(2)}) collective-permute-start(bf16[2,512,256]{2,1,0:T(8,128)(2,1)} %collective-permute-done.13.refs_10_), channel_id=1, source_target_pairs={{0,7},{1,0},{2,1},{3,2},{4,3},{5,4},{6,5},{7,6},{8,15},{9,8},{10,9... | collective-permute-start | bytes 1572872 | tf_op jit(solution)/shard_map/ppermute | solution.py:85
  98.8 10.5 %collective-permute-start.24 = (bf16[2,512,256]{2,1,0:T(8,128)(2,1)}, bf16[2,512,256]{2,1,0:T(8,128)(2,1)}, u32[]{:S(2)}, u32[]{:S(2)}) collective-permute-start(bf16[2,512,256]{2,1,0:T(8,128)(2,1)} %collective-permute-done.16.refs_13_), channel_id=1, source_target_pairs={{32,56},{33,57},{34,58},{35,59},{36,60},{37,61},{38,62},{39,63},{4... | collective-permute-start | bytes 1572872 | tf_op jit(solution)/shard_map/ppermute | solution.py:85
  100.8 8.6 %collective-permute-start.18 = (bf16[2,512,256]{2,1,0:T(8,128)(2,1)}, bf16[2,512,256]{2,1,0:T(8,128)(2,1)}, u32[]{:S(2)}, u32[]{:S(2)}) collective-permute-start(bf16[2,512,256]{2,1,0:T(8,128)(2,1)} %collective-permute-done.12.refs_9_), channel_id=1, source_target_pairs={{0,1},{1,2},{2,3},{3,4},{4,5},{5,6},{6,7},{7,0},{8,9},{9,10},{10,1... | collective-permute-start | bytes 1572872 | tf_op jit(solution)/shard_map/ppermute | solution.py:85
  102.3 7.1 %collective-permute-start.25 = (bf16[2,512,256]{2,1,0:T(8,128)(2,1)}, bf16[2,512,256]{2,1,0:T(8,128)(2,1)}, u32[]{:S(2)}, u32[]{:S(2)}) collective-permute-start(bf16[2,512,256]{2,1,0:T(8,128)(2,1)} %collective-permute-done.17.refs_14_), channel_id=1, source_target_pairs={{0,1},{1,2},{2,3},{3,4},{4,5},{5,6},{6,7},{7,0},{8,9},{9,10},{10,1... | collective-permute-start | bytes 1572872 | tf_op jit(solution)/shard_map/ppermute | solution.py:85
  103.7 5.6 %collective-permute-start.26 = (bf16[2,512,256]{2,1,0:T(8,128)(2,1)}, bf16[2,512,256]{2,1,0:T(8,128)(2,1)}, u32[]{:S(2)}, u32[]{:S(2)}) collective-permute-start(bf16[2,512,256]{2,1,0:T(8,128)(2,1)} %collective-permute-done.22.refs_19_), channel_id=1, source_target_pairs={{0,7},{1,0},{2,1},{3,2},{4,3},{5,4},{6,5},{7,6},{8,15},{9,8},{10,9... | collective-permute-start | bytes 1572872 | tf_op jit(solution)/shard_map/ppermute | solution.py:85
  113.7 1.3 copy-start
  115.1 15.7 %all-to-all-start.1 = ((bf16[8,64,512]{2,1,0:T(8,128)(2,1)}), bf16[8,64,512]{2,1,0:T(8,128)(2,1)S(1)}, u32[]{:S(2)}, u32[]{:S(2)}) async-start(bf16[8,64,512]{2,1,0:T(8,128)(2,1)} %get-tuple-element.8), calls=%async_computation.1 | async-start | bytes 1048576 | tf_op jit(solution)/shard_map/all_to_all | solution.py:329
  146.6 11.4 %collective-permute-start.27 = (bf16[8,64,256]{2,1,0:T(8,128)(2,1)S(1)}, bf16[8,64,256]{2,1,0:T(8,128)(2,1)S(1)}, u32[]{:S(2)}, u32[]{:S(2)}) collective-permute-start(bf16[8,64,256]{2,1,0:T(8,128)(2,1)S(1)} %shard_map.62.own_ref), channel_id=1, source_target_pairs={{0,32},{32,0},{1,33},{33,1},{2,34},{34,2},{3,35},{35,3},{4,36},{36... | collective-permute-start | bytes 786440 | tf_op jit(solution)/shard_map/ppermute | solution.py:359
  159.4 52.2 %copy-start.1 = (bf16[8,512,256]{2,1,0:T(8,128)(2,1)S(1)}, bf16[8,512,256]{2,1,0:T(8,128)(2,1)}, u32[]{:S(2)}) copy-start(bf16[8,512,256]{2,1,0:T(8,128)(2,1)} %copy-done) | copy-start | bytes 6291460
  213.0 4.2 %collective-permute-start.28 = (bf16[8,64,128]{2,1,0:T(8,128)(2,1)S(1)}, bf16[8,64,128]{2,1,0:T(8,128)(2,1)S(1)}, u32[]{:S(2)}, u32[]{:S(2)}) collective-permute-start(bf16[8,64,128]{2,1,0:T(8,128)(2,1)S(1)} %get-tuple-element.13), channel_id=1, source_target_pairs={{0,32},{32,0},{1,33},{33,1},{2,34},{34,2},{3,35},{35,3},{4,36},{36... | collective-permute-start | bytes 393224 | tf_op jit(solution)/shard_map/ppermute | solution.py:374
where the time goes:
time: 221 us; the launch traced here: 218 us
  starting transfers between devices  85 us (38%)
  blocking collectives  84.4 us (38%)
  waiting for transfers between devices  25.2 us (11%)
  Pallas kernels  15.8 us (7%)
  other arithmetic  4.14 us (2%)
    all_to_all x4, blocking collectives, exchange(): return lax.all_to_all(x, 'z', 0, 0, tiled=True)  84.4 us
    ppermute x20, starting transfers between devices, bundle_send(): return lax.ppermute(value, ('core', 'x', 'y'), pairs)  45.8 us
    ppermute x7, starting transfers between devices, send(): return lax.ppermute(value, ('core', 'x', 'y'), pairs)  22.2 us
    pallas_call x7, Pallas kernels, call(): pl.pallas_call(kernel, out_shape=out_shape, in_specs=in_specs, out_specs=...  15.8 us
    all_to_all x1, waiting for transfers between devices, exchange(): return lax.all_to_all(x, 'z', 0, 0, tiled=True)  12 us
    ppermute x1, starting transfers between devices, local(): other = lax.ppermute(own, 'core', swap)  10.3 us
    ppermute x20, waiting for transfers between devices, bundle_send(): return lax.ppermute(value, ('core', 'x', 'y'), pairs)  5.68 us
    ppermute x7, waiting for transfers between devices, send(): return lax.ppermute(value, ('core', 'x', 'y'), pairs)  5.44 us
  transfers between devices with their start and end apart: 30, of which 10 were waited for; matrix products, arithmetic and copies ran while one was open for 2% of the time, Pallas kernels for 0%

commit v1 on v0

--- a/solution.py
+++ b/solution.py
@@ -104,9 +104,9 @@
         b5[h] = bundle_send(far[h], None, 1)
         a6[h] = bundle_send(a4[h], -1, None)
         b6[h] = bundle_send(b4[h], None, -1)
-    out7 = bundle_send(a5[0], 1, None)
-    out8 = bundle_send(a6[1], -1, None)
-    return (*near, *far, *out1, *out2, *out3, *a4, *b4, *a5, *b5, *a6, *b6, out7, out8)
+    out7 = bundle_send(a5[1], 1, None)
+    out8 = bundle_send(a6[0], -1, None)
+    return (*near, *far, *out1, *out2, *out3, *a4, *b4, *a5, *b5, *a6, *b6, out8, out7)
 
 
 def pick(index, *values):
@@ -306,7 +306,7 @@
     side = lax.axis_index("core").astype(jnp.int32).reshape(1)
     row_first = tile_list[:, 0].astype(jnp.int32)
     row_second = tile_list[:, 1].astype(jnp.int32)
-    params = pltpu.CompilerParams(vmem_limit_bytes=32 * 1024 * 1024)
+    params = pltpu.CompilerParams(vmem_limit_bytes=12 * 1024 * 1024)
 
     smem = pl.BlockSpec(memory_space=pltpu.SMEM)
     hbm = pl.BlockSpec(memory_space=pl.ANY)

time: 221 us -> 227 us (1.027)
  the two profiles are of different devices: /device:TPU:1 before, /device:TPU:25 now
where the time goes in v1:
time: 227 us; the launch traced here: 226 us
  blocking collectives  89.3 us (39%)
  starting transfers between devices  80.5 us (35%)
  waiting for transfers between devices  32.9 us (14%)
  Pallas kernels  15.8 us (7%)
  other arithmetic  4.21 us (2%)
    all_to_all x4, blocking collectives, exchange(): return lax.all_to_all(x, 'z', 0, 0, tiled=True)  89.3 us
    ppermute x20, starting transfers between devices, bundle_send(): return lax.ppermute(value, ('core', 'x', 'y'), pairs)  45.8 us
    ppermute x7, starting transfers between devices, send(): return lax.ppermute(value, ('core', 'x', 'y'), pairs)  25.5 us
    all_to_all x1, waiting for transfers between devices, exchange(): return lax.all_to_all(x, 'z', 0, 0, tiled=True)  17.8 us
    pallas_call x7, Pallas kernels, call(): pl.pallas_call(kernel, out_shape=out_shape, in_specs=in_specs, out_specs=...  15.8 us
    ppermute x20, waiting for transfers between devices, bundle_send(): return lax.ppermute(value, ('core', 'x', 'y'), pairs)  8.87 us
  transfers between devices with their start and end apart: 30, of which 10 were waited for; matrix products, arithmetic and copies ran while one was open for 2% of the time, Pallas kernels for 0%

profile of v1, /device:TPU:25, one launch (start us, length us, event | category | flops | bytes accessed | tf_op | source)
XLA Modules:
  0.0 226.0 jit_solution(8792473203325354881)
XLA Ops:
  2.3 23.4 %all_to_all.25 = bf16[8,64,384]{2,1,0:T(8,128)(2,1)S(1)} all-to-all(bf16[8,64,384]{2,1,0:T(8,128)(2,1)S(1)} %shard_map.59), channel_id=1, replica_groups=mesh['z'=8,'core'=2,'x'=4,'y'=8] {'z'}, dimensions={0} | all-to-all | bytes 786432 | tf_op jit(solution)/shard_map/all_to_all | solution.py:329
  25.8 4.4 %collective-permute-start = (bf16[512,256]{1,0:T(8,128)(2,1)S(1)}, bf16[512,256]{1,0:T(8,128)(2,1)S(1)}, u32[]{:S(2)}, u32[]{:S(2)}) collective-permute-start(bf16[512,256]{1,0:T(8,128)(2,1)S(1)} %bitcast.57), channel_id=1, source_target_pairs={{0,8},{32,33},{1,9},{33,34},{2,10},{34,35},{3,11},{35,36},{4,12},{... | collective-permute-start | bytes 786440 | tf_op jit(solution)/shard_map/ppermute | solution.py:75
  30.2 1.9 collective-permute-start.1
  32.1 1.4 collective-permute-done
  33.5 5.3 %collective-permute-start.2 = (bf16[512,256]{1,0:T(8,128)(2,1)S(1)}, bf16[512,256]{1,0:T(8,128)(2,1)S(1)}, u32[]{:S(2)}, u32[]{:S(2)}) collective-permute-start(bf16[512,256]{1,0:T(8,128)(2,1)S(1)} %collective-permute-done), channel_id=1, source_target_pairs={{0,8},{32,33},{1,9},{33,34},{2,10},{34,35},{3,11},{35,36},{4,12},{... | collective-permute-start | bytes 786440 | tf_op jit(solution)/shard_map/ppermute | solution.py:75
  38.8 1.9 collective-permute-start.3
  40.7 1.4 collective-permute-done.2
  42.1 5.0 %collective-permute-start.4 = (bf16[512,256]{1,0:T(8,128)(2,1)S(1)}, bf16[512,256]{1,0:T(8,128)(2,1)S(1)}, u32[]{:S(2)}, u32[]{:S(2)}) collective-permute-start(bf16[512,256]{1,0:T(8,128)(2,1)S(1)} %collective-permute-done.2), channel_id=1, source_target_pairs={{32,33},{33,34},{34,35},{35,36},{36,37},{37,38},{38,39},{39,32},{4... | collective-permute-start | bytes 786440 | tf_op jit(solution)/shard_map/ppermute | solution.py:75
  47.1 1.9 collective-permute-start.5
  49.1 1.4 collective-permute-done.4
  50.4 5.0 %collective-permute-start.6 = (bf16[512,256]{1,0:T(8,128)(2,1)S(1)}, bf16[512,256]{1,0:T(8,128)(2,1)S(1)}, u32[]{:S(2)}, u32[]{:S(2)}) collective-permute-start(bf16[512,256]{1,0:T(8,128)(2,1)S(1)} %collective-permute-done.4), channel_id=1, source_target_pairs={{32,33},{33,34},{34,35},{35,36},{36,37},{37,38},{38,39},{39,32},{4... | collective-permute-start | bytes 786440 | tf_op jit(solution)/shard_map/ppermute | solution.py:75
  55.5 4.1 %collective-permute-start.9 = (bf16[2,512,256]{2,1,0:T(8,128)(2,1)S(1)}, bf16[2,512,256]{2,1,0:T(8,128)(2,1)S(1)}, u32[]{:S(2)}, u32[]{:S(2)}) collective-permute-start(bf16[2,512,256]{2,1,0:T(8,128)(2,1)S(1)} %pad_maximum_fusion.refs_0_), channel_id=1, source_target_pairs={{0,7},{32,56},{1,0},{33,57},{2,1},{34,58},{3,2},{35,59},{4,3},{36,... | collective-permute-start | bytes 1572872 | tf_op jit(solution)/shard_map/ppermute | solution.py:85
  59.6 1.9 collective-permute-start.7
  61.6 4.6 %collective-permute-start.10 = (bf16[2,512,256]{2,1,0:T(8,128)(2,1)S(1)}, bf16[2,512,256]{2,1,0:T(8,128)(2,1)S(1)}, u32[]{:S(2)}, u32[]{:S(2)}) collective-permute-start(bf16[2,512,256]{2,1,0:T(8,128)(2,1)S(1)} %pad_maximum_fusion.1.refs_1_), channel_id=1, source_target_pairs={{0,7},{32,56},{1,0},{33,57},{2,1},{34,58},{3,2},{35,59},{4,3},{36,... | collective-permute-start | bytes 1572872 | tf_op jit(solution)/shard_map/ppermute | solution.py:85
  66.3 1.9 collective-permute-start.8
  68.2 1.9 collective-permute-start.19
  70.2 4.6 %collective-permute-start.15 = (bf16[2,512,256]{2,1,0:T(8,128)(2,1)S(1)}, bf16[2,512,256]{2,1,0:T(8,128)(2,1)}, u32[]{:S(2)}, u32[]{:S(2)}) collective-permute-start(bf16[2,512,256]{2,1,0:T(8,128)(2,1)S(1)} %pad_maximum_fusion.2.refs_2_), channel_id=1, source_target_pairs={{32,56},{33,57},{34,58},{35,59},{36,60},{37,61},{38,62},{39,63},{4... | collective-permute-start | bytes 1572872 | tf_op jit(solution)/shard_map/ppermute | solution.py:85
  74.8 1.5 collective-permute-start.13
  76.3 1.9 collective-permute-start.11
  78.3 2.8 %collective-permute-start.20 = (bf16[2,512,256]{2,1,0:T(8,128)(2,1)S(1)}, bf16[2,512,256]{2,1,0:T(8,128)(2,1)S(1)}, u32[]{:S(2)}, u32[]{:S(2)}) collective-permute-start(bf16[2,512,256]{2,1,0:T(8,128)(2,1)S(1)} %pad_maximum_fusion.3.refs_3_), channel_id=1, source_target_pairs={{32,40},{33,41},{34,42},{35,43},{36,44},{37,45},{38,46},{39,47},{4... | collective-permute-start | bytes 1572872 | tf_op jit(solution)/shard_map/ppermute | solution.py:85
  81.0 2.0 collective-permute-done.19.refs_16_
  83.0 1.9 collective-permute-start.12
  85.0 4.6 %collective-permute-start.16 = (bf16[2,512,256]{2,1,0:T(8,128)(2,1)S(1)}, bf16[2,512,256]{2,1,0:T(8,128)(2,1)}, u32[]{:S(2)}, u32[]{:S(2)}) collective-permute-start(bf16[2,512,256]{2,1,0:T(8,128)(2,1)S(1)} %pad_maximum_fusion.3.refs_3_), channel_id=1, source_target_pairs={{32,56},{33,57},{34,58},{35,59},{36,60},{37,61},{38,62},{39,63},{4... | collective-permute-start | bytes 1572872 | tf_op jit(solution)/shard_map/ppermute | solution.py:85
  89.6 1.5 collective-permute-start.14
  91.0 1.9 collective-permute-start.23
  92.9 1.7 collective-permute-done.20.refs_17_
  94.7 1.5 collective-permute-start.21
  96.1 3.8 %collective-permute-done.12.refs_9_ = bf16[2,512,256]{2,1,0:T(8,128)(2,1)} collective-permute-done((bf16[2,512,256]{2,1,0:T(8,128)(2,1)S(1)}, bf16[2,512,256]{2,1,0:T(8,128)(2,1)}, u32[]{:S(2)}, u32[]{:S(2)}) %collective-permute-start.12) | collective-permute-done | bytes 524320 | tf_op jit(solution)/shard_map/ppermute | solution.py:85
  100.0 1.5 collective-permute-start.18
  102.0 1.5 collective-permute-start.17
  103.6 1.9 collective-permute-start.24
  105.5 1.5 collective-permute-start.22
  107.0 1.5 collective-permute-start.25
  108.4 1.5 collective-permute-start.26
  112.5 1.3 collective-permute-done.24.refs_21_
  113.9 4.3 %shard_map.60 = (bf16[8,64,512]{2,1,0:T(8,128)(2,1)}, bf16[8,512,256]{2,1,0:T(8,128)(2,1)S(1)}, bf16[8,512,256]{2,1,0:T(8,128)(2,1)S(1)}) custom-call(s32[2,8]{1,0:T(2,128)S(1)} %pad_add_fusion.first_ref, s32[2,8]{1,0:T(2,128)S(1)} %pad_add_fusion.1.second_ref, s32[1]{0:T(128)} %bitcast.3.z_ref, bf16[8,64,2048]{2,1,0:T(8,128)(2,1)} %bitcast.56, ...), custom_call_target="tpu_custom_call" | custom-call | tf_op jit(solution)/shard_map/pallas_call | solution.py:316
  118.2 1.3 copy-done
  119.5 3.5 %all-to-all-start.1 = ((bf16[8,64,512]{2,1,0:T(8,128)(2,1)}), bf16[8,64,512]{2,1,0:T(8,128)(2,1)S(1)}, u32[]{:S(2)}, u32[]{:S(2)}) async-start(bf16[8,64,512]{2,1,0:T(8,128)(2,1)} %get-tuple-element.8), calls=%async_computation.1 | async-start | bytes 1048576 | tf_op jit(solution)/shard_map/all_to_all | solution.py:329
  123.2 17.8 %all-to-all-done.1.part_ref = bf16[8,64,512]{2,1,0:T(8,128)(2,1)S(1)} async-done(((bf16[8,64,512]{2,1,0:T(8,128)(2,1)}), bf16[8,64,512]{2,1,0:T(8,128)(2,1)S(1)}, u32[]{:S(2)}, u32[]{:S(2)}) %all-to-all-start.1) | async-done | bytes 524320 | tf_op jit(solution)/shard_map/all_to_all | solution.py:329
  141.7 20.3 %all_to_all.26.core_ref = bf16[8,64,512]{2,1,0:T(8,128)(2,1)S(1)} all-to-all(bf16[8,64,512]{2,1,0:T(8,128)(2,1)S(1)} %shard_map.61), channel_id=1, replica_groups=mesh['z'=8,'core'=2,'x'=4,'y'=8] {'z'}, dimensions={0} | all-to-all | bytes 1048576 | tf_op jit(solution)/shard_map/all_to_all | solution.py:329
  162.5 2.4 %collective-permute-start.27 = (bf16[8,64,256]{2,1,0:T(8,128)(2,1)S(1)}, bf16[8,64,256]{2,1,0:T(8,128)(2,1)S(1)}, u32[]{:S(2)}, u32[]{:S(2)}) collective-permute-start(bf16[8,64,256]{2,1,0:T(8,128)(2,1)S(1)} %shard_map.62.own_ref), channel_id=1, source_target_pairs={{0,32},{32,0},{1,33},{33,1},{2,34},{34,2},{3,35},{35,3},{4,36},{36... | collective-permute-start | bytes 786440 | tf_op jit(solution)/shard_map/ppermute | solution.py:359
  164.9 1.1 collective-permute-done.27.other_ref
  166.1 1.4 shard_map.63
  167.5 23.3 %all_to_all.27.part_ref = bf16[8,80,512]{2,1,0:T(8,128)(2,1)S(1)} all-to-all(bf16[8,80,512]{2,1,0:T(8,128)(2,1)S(1)} %shard_map.63), channel_id=1, replica_groups=mesh['z'=8,'core'=2,'x'=4,'y'=8] {'z'}, dimensions={0} | all-to-all | bytes 1310720 | tf_op jit(solution)/shard_map/all_to_all | solution.py:329
  190.7 6.6 %shard_map.64 = bf16[8,80,512]{2,1,0:T(8,128)(2,1)S(1)} custom-call(bf16[8,80,512]{2,1,0:T(8,128)(2,1)S(1)} %all_to_all.27.part_ref, f32[8,64,64]{2,1,0:T(8,128)S(1)} %slice_add_fusion.cores_ref), custom_call_target="tpu_custom_call" | custom-call | tf_op jit(solution)/shard_map/pallas_call | solution.py:316
  197.3 22.3 %all_to_all.28.core_ref = bf16[8,80,512]{2,1,0:T(8,128)(2,1)S(1)} all-to-all(bf16[8,80,512]{2,1,0:T(8,128)(2,1)S(1)} %shard_map.64), channel_id=1, replica_groups=mesh['z'=8,'core'=2,'x'=4,'y'=8] {'z'}, dimensions={0} | all-to-all | bytes 1310720 | tf_op jit(solution)/shard_map/all_to_all | solution.py:329
  219.6 1.4 shard_map.65
  221.0 3.3 %collective-permute-start.28 = (bf16[8,64,128]{2,1,0:T(8,128)(2,1)S(1)}, bf16[8,64,128]{2,1,0:T(8,128)(2,1)S(1)}, u32[]{:S(2)}, u32[]{:S(2)}) collective-permute-start(bf16[8,64,128]{2,1,0:T(8,128)(2,1)S(1)} %get-tuple-element.13), channel_id=1, source_target_pairs={{0,32},{32,0},{1,33},{33,1},{2,34},{34,2},{3,35},{35,3},{4,36},{36... | collective-permute-start | bytes 393224 | tf_op jit(solution)/shard_map/ppermute | solution.py:374
  (64 shorter events, 8.2 us)
Async XLA Ops:
  0.6 0.8 copy-start.2
  25.8 7.7 %collective-permute-start = (bf16[512,256]{1,0:T(8,128)(2,1)S(1)}, bf16[512,256]{1,0:T(8,128)(2,1)S(1)}, u32[]{:S(2)}, u32[]{:S(2)}) collective-permute-start(bf16[512,256]{1,0:T(8,128)(2,1)S(1)} %bitcast.57), channel_id=1, source_target_pairs={{0,8},{32,33},{1,9},{33,34},{2,10},{34,35},{3,11},{35,36},{4,12},{... | collective-permute-start | bytes 786440 | tf_op jit(solution)/shard_map/ppermute | solution.py:75
  30.2 8.6 %collective-permute-start.1 = (bf16[512,256]{1,0:T(8,128)(2,1)S(1)}, bf16[512,256]{1,0:T(8,128)(2,1)S(1)}, u32[]{:S(2)}, u32[]{:S(2)}) collective-permute-start(bf16[512,256]{1,0:T(8,128)(2,1)S(1)} %bitcast.58), channel_id=1, source_target_pairs={{0,24},{32,39},{1,25},{33,32},{2,26},{34,33},{3,27},{35,34},{4,28}... | collective-permute-start | bytes 786440 | tf_op jit(solution)/shard_map/ppermute | solution.py:75
  33.5 8.6 %collective-permute-start.2 = (bf16[512,256]{1,0:T(8,128)(2,1)S(1)}, bf16[512,256]{1,0:T(8,128)(2,1)S(1)}, u32[]{:S(2)}, u32[]{:S(2)}) collective-permute-start(bf16[512,256]{1,0:T(8,128)(2,1)S(1)} %collective-permute-done), channel_id=1, source_target_pairs={{0,8},{32,33},{1,9},{33,34},{2,10},{34,35},{3,11},{35,36},{4,12},{... | collective-permute-start | bytes 786440 | tf_op jit(solution)/shard_map/ppermute | solution.py:75
  38.8 8.3 %collective-permute-start.3 = (bf16[512,256]{1,0:T(8,128)(2,1)S(1)}, bf16[512,256]{1,0:T(8,128)(2,1)S(1)}, u32[]{:S(2)}, u32[]{:S(2)}) collective-permute-start(bf16[512,256]{1,0:T(8,128)(2,1)S(1)} %collective-permute-done.1), channel_id=1, source_target_pairs={{32,39},{33,32},{34,33},{35,34},{36,35},{37,36},{38,37},{39,38},{4... | collective-permute-start | bytes 786440 | tf_op jit(solution)/shard_map/ppermute | solution.py:75
  42.1 8.3 %collective-permute-start.4 = (bf16[512,256]{1,0:T(8,128)(2,1)S(1)}, bf16[512,256]{1,0:T(8,128)(2,1)S(1)}, u32[]{:S(2)}, u32[]{:S(2)}) collective-permute-start(bf16[512,256]{1,0:T(8,128)(2,1)S(1)} %collective-permute-done.2), channel_id=1, source_target_pairs={{32,33},{33,34},{34,35},{35,36},{36,37},{37,38},{38,39},{39,32},{4... | collective-permute-start | bytes 786440 | tf_op jit(solution)/shard_map/ppermute | solution.py:75
  47.1 19.1 %collective-permute-start.5 = (bf16[512,256]{1,0:T(8,128)(2,1)S(1)}, bf16[512,256]{1,0:T(8,128)(2,1)S(1)}, u32[]{:S(2)}, u32[]{:S(2)}) collective-permute-start(bf16[512,256]{1,0:T(8,128)(2,1)S(1)} %collective-permute-done.3), channel_id=1, source_target_pairs={{32,39},{33,32},{34,33},{35,34},{36,35},{37,36},{38,37},{39,38},{4... | collective-permute-start | bytes 786440 | tf_op jit(solution)/shard_map/ppermute | solution.py:75
  50.4 17.8 %collective-permute-start.6 = (bf16[512,256]{1,0:T(8,128)(2,1)S(1)}, bf16[512,256]{1,0:T(8,128)(2,1)S(1)}, u32[]{:S(2)}, u32[]{:S(2)}) collective-permute-start(bf16[512,256]{1,0:T(8,128)(2,1)S(1)} %collective-permute-done.4), channel_id=1, source_target_pairs={{32,33},{33,34},{34,35},{35,36},{36,37},{37,38},{38,39},{39,32},{4... | collective-permute-start | bytes 786440 | tf_op jit(solution)/shard_map/ppermute | solution.py:75
  55.4 46.1 %copy-start.13 = (s32[8,2]{0,1:T(2,128)S(1)}, s32[8,2]{0,1:T(2,128)}, u32[]{:S(2)}) copy-start(s32[8,2]{0,1:T(2,128)} %param.6) | copy-start | bytes 196
  55.5 58.3 %copy-start.3 = (bf16[2,512,256]{2,1,0:T(8,128)(2,1)}, bf16[2,512,256]{2,1,0:T(8,128)(2,1)S(1)}, u32[]{:S(2)}) copy-start(bf16[2,512,256]{2,1,0:T(8,128)(2,1)S(1)} %pad_maximum_fusion.refs_0_) | copy-start | bytes 1572868
  55.5 14.7 %collective-permute-start.9 = (bf16[2,512,256]{2,1,0:T(8,128)(2,1)S(1)}, bf16[2,512,256]{2,1,0:T(8,128)(2,1)S(1)}, u32[]{:S(2)}, u32[]{:S(2)}) collective-permute-start(bf16[2,512,256]{2,1,0:T(8,128)(2,1)S(1)} %pad_maximum_fusion.refs_0_), channel_id=1, source_target_pairs={{0,7},{32,56},{1,0},{33,57},{2,1},{34,58},{3,2},{35,59},{4,3},{36,... | collective-permute-start | bytes 1572872 | tf_op jit(solution)/shard_map/ppermute | solution.py:85
  59.6 15.2 %collective-permute-start.7 = (bf16[2,512,256]{2,1,0:T(8,128)(2,1)S(1)}, bf16[2,512,256]{2,1,0:T(8,128)(2,1)S(1)}, u32[]{:S(2)}, u32[]{:S(2)}) collective-permute-start(bf16[2,512,256]{2,1,0:T(8,128)(2,1)S(1)} %pad_maximum_fusion.refs_0_), channel_id=1, source_target_pairs={{0,1},{32,40},{1,2},{33,41},{2,3},{34,42},{3,4},{35,43},{4,5},{36,... | collective-permute-start | bytes 1572872 | tf_op jit(solution)/shard_map/ppermute | solution.py:85
  61.6 52.2 %copy-start.4 = (bf16[2,512,256]{2,1,0:T(8,128)(2,1)}, bf16[2,512,256]{2,1,0:T(8,128)(2,1)S(1)}, u32[]{:S(2)}) copy-start(bf16[2,512,256]{2,1,0:T(8,128)(2,1)S(1)} %pad_maximum_fusion.1.refs_1_) | copy-start | bytes 1572868
  61.6 14.7 %collective-permute-start.10 = (bf16[2,512,256]{2,1,0:T(8,128)(2,1)S(1)}, bf16[2,512,256]{2,1,0:T(8,128)(2,1)S(1)}, u32[]{:S(2)}, u32[]{:S(2)}) collective-permute-start(bf16[2,512,256]{2,1,0:T(8,128)(2,1)S(1)} %pad_maximum_fusion.1.refs_1_), channel_id=1, source_target_pairs={{0,7},{32,56},{1,0},{33,57},{2,1},{34,58},{3,2},{35,59},{4,3},{36,... | collective-permute-start | bytes 1572872 | tf_op jit(solution)/shard_map/ppermute | solution.py:85
  66.3 12.0 %copy-start.5 = (bf16[2,512,256]{2,1,0:T(8,128)(2,1)}, bf16[2,512,256]{2,1,0:T(8,128)(2,1)S(1)}, u32[]{:S(2)}) copy-start(bf16[2,512,256]{2,1,0:T(8,128)(2,1)S(1)} %pad_maximum_fusion.2.refs_2_) | copy-start | bytes 1572868
  66.3 12.0 %collective-permute-start.8 = (bf16[2,512,256]{2,1,0:T(8,128)(2,1)S(1)}, bf16[2,512,256]{2,1,0:T(8,128)(2,1)S(1)}, u32[]{:S(2)}, u32[]{:S(2)}) collective-permute-start(bf16[2,512,256]{2,1,0:T(8,128)(2,1)S(1)} %pad_maximum_fusion.1.refs_1_), channel_id=1, source_target_pairs={{0,1},{32,40},{1,2},{33,41},{2,3},{34,42},{3,4},{35,43},{4,5},{36,... | collective-permute-start | bytes 1572872 | tf_op jit(solution)/shard_map/ppermute | solution.py:85
  68.2 14.8 %collective-permute-start.19 = (bf16[2,512,256]{2,1,0:T(8,128)(2,1)S(1)}, bf16[2,512,256]{2,1,0:T(8,128)(2,1)S(1)}, u32[]{:S(2)}, u32[]{:S(2)}) collective-permute-start(bf16[2,512,256]{2,1,0:T(8,128)(2,1)S(1)} %pad_maximum_fusion.2.refs_2_), channel_id=1, source_target_pairs={{32,40},{33,41},{34,42},{35,43},{36,44},{37,45},{38,46},{39,47},{4... | collective-permute-start | bytes 1572872 | tf_op jit(solution)/shard_map/ppermute | solution.py:85
  70.2 43.6 %copy-start.6 = (bf16[2,512,256]{2,1,0:T(8,128)(2,1)}, bf16[2,512,256]{2,1,0:T(8,128)(2,1)S(1)}, u32[]{:S(2)}) copy-start(bf16[2,512,256]{2,1,0:T(8,128)(2,1)S(1)} %pad_maximum_fusion.3.refs_3_) | copy-start | bytes 1572868
  70.2 43.6 %copy-start.7 = (bf16[2,512,256]{2,1,0:T(8,128)(2,1)}, bf16[2,512,256]{2,1,0:T(8,128)(2,1)S(1)}, u32[]{:S(2)}) copy-start(bf16[2,512,256]{2,1,0:T(8,128)(2,1)S(1)} %collective-permute-done.9.refs_6_) | copy-start | bytes 1572868
  70.2 14.7 %collective-permute-start.15 = (bf16[2,512,256]{2,1,0:T(8,128)(2,1)S(1)}, bf16[2,512,256]{2,1,0:T(8,128)(2,1)}, u32[]{:S(2)}, u32[]{:S(2)}) collective-permute-start(bf16[2,512,256]{2,1,0:T(8,128)(2,1)S(1)} %pad_maximum_fusion.2.refs_2_), channel_id=1, source_target_pairs={{32,56},{33,57},{34,58},{35,59},{36,60},{37,61},{38,62},{39,63},{4... | collective-permute-start | bytes 1572872 | tf_op jit(solution)/shard_map/ppermute | solution.py:85
  74.8 39.0 %copy-start.8 = (bf16[2,512,256]{2,1,0:T(8,128)(2,1)}, bf16[2,512,256]{2,1,0:T(8,128)(2,1)S(1)}, u32[]{:S(2)}) copy-start(bf16[2,512,256]{2,1,0:T(8,128)(2,1)S(1)} %collective-permute-done.7.refs_4_) | copy-start | bytes 1572868
  74.8 14.7 %collective-permute-start.13 = (bf16[2,512,256]{2,1,0:T(8,128)(2,1)S(1)}, bf16[2,512,256]{2,1,0:T(8,128)(2,1)}, u32[]{:S(2)}, u32[]{:S(2)}) collective-permute-start(bf16[2,512,256]{2,1,0:T(8,128)(2,1)S(1)} %collective-permute-done.9.refs_6_), channel_id=1, source_target_pairs={{0,7},{1,0},{2,1},{3,2},{4,3},{5,4},{6,5},{7,6},{8,15},{9,8},{10,9... | collective-permute-start | bytes 1572872 | tf_op jit(solution)/shard_map/ppermute | solution.py:85
  76.3 37.5 %copy-start.9 = (bf16[2,512,256]{2,1,0:T(8,128)(2,1)}, bf16[2,512,256]{2,1,0:T(8,128)(2,1)S(1)}, u32[]{:S(2)}) copy-start(bf16[2,512,256]{2,1,0:T(8,128)(2,1)S(1)} %collective-permute-done.10.refs_7_) | copy-start | bytes 1572868
  76.3 14.7 %collective-permute-start.11 = (bf16[2,512,256]{2,1,0:T(8,128)(2,1)S(1)}, bf16[2,512,256]{2,1,0:T(8,128)(2,1)}, u32[]{:S(2)}, u32[]{:S(2)}) collective-permute-start(bf16[2,512,256]{2,1,0:T(8,128)(2,1)S(1)} %collective-permute-done.7.refs_4_), channel_id=1, source_target_pairs={{0,1},{32,40},{1,2},{33,41},{2,3},{34,42},{3,4},{35,43},{4,5},{36,... | collective-permute-start | bytes 1572872 | tf_op jit(solution)/shard_map/ppermute | solution.py:85
  78.3 16.4 %copy-start.10 = (bf16[2,512,256]{2,1,0:T(8,128)(2,1)}, bf16[2,512,256]{2,1,0:T(8,128)(2,1)S(1)}, u32[]{:S(2)}) copy-start(bf16[2,512,256]{2,1,0:T(8,128)(2,1)S(1)} %collective-permute-done.8.refs_5_) | copy-start | bytes 1572868
  78.3 16.4 %collective-permute-start.20 = (bf16[2,512,256]{2,1,0:T(8,128)(2,1)S(1)}, bf16[2,512,256]{2,1,0:T(8,128)(2,1)S(1)}, u32[]{:S(2)}, u32[]{:S(2)}) collective-permute-start(bf16[2,512,256]{2,1,0:T(8,128)(2,1)S(1)} %pad_maximum_fusion.3.refs_3_), channel_id=1, source_target_pairs={{32,40},{33,41},{34,42},{35,43},{36,44},{37,45},{38,46},{39,47},{4... | collective-permute-start | bytes 1572872 | tf_op jit(solution)/shard_map/ppermute | solution.py:85
  83.0 17.0 %copy-start.11 = (bf16[2,512,256]{2,1,0:T(8,128)(2,1)}, bf16[2,512,256]{2,1,0:T(8,128)(2,1)S(1)}, u32[]{:S(2)}) copy-start(bf16[2,512,256]{2,1,0:T(8,128)(2,1)S(1)} %collective-permute-done.19.refs_16_) | copy-start | bytes 1572868
  83.0 17.0 %collective-permute-start.12 = (bf16[2,512,256]{2,1,0:T(8,128)(2,1)S(1)}, bf16[2,512,256]{2,1,0:T(8,128)(2,1)}, u32[]{:S(2)}, u32[]{:S(2)}) collective-permute-start(bf16[2,512,256]{2,1,0:T(8,128)(2,1)S(1)} %collective-permute-done.8.refs_5_), channel_id=1, source_target_pairs={{0,1},{32,40},{1,2},{33,41},{2,3},{34,42},{3,4},{35,43},{4,5},{36,... | collective-permute-start | bytes 1572872 | tf_op jit(solution)/shard_map/ppermute | solution.py:85
  85.0 17.1 %collective-permute-start.16 = (bf16[2,512,256]{2,1,0:T(8,128)(2,1)S(1)}, bf16[2,512,256]{2,1,0:T(8,128)(2,1)}, u32[]{:S(2)}, u32[]{:S(2)}) collective-permute-start(bf16[2,512,256]{2,1,0:T(8,128)(2,1)S(1)} %pad_maximum_fusion.3.refs_3_), channel_id=1, source_target_pairs={{32,56},{33,57},{34,58},{35,59},{36,60},{37,61},{38,62},{39,63},{4... | collective-permute-start | bytes 1572872 | tf_op jit(solution)/shard_map/ppermute | solution.py:85
  89.6 14.0 %collective-permute-start.14 = (bf16[2,512,256]{2,1,0:T(8,128)(2,1)S(1)}, bf16[2,512,256]{2,1,0:T(8,128)(2,1)}, u32[]{:S(2)}, u32[]{:S(2)}) collective-permute-start(bf16[2,512,256]{2,1,0:T(8,128)(2,1)S(1)} %collective-permute-done.10.refs_7_), channel_id=1, source_target_pairs={{0,7},{1,0},{2,1},{3,2},{4,3},{5,4},{6,5},{7,6},{8,15},{9,8},{10,9... | collective-permute-start | bytes 1572872 | tf_op jit(solution)/shard_map/ppermute | solution.py:85
  91.0 14.4 %collective-permute-start.23 = (bf16[2,512,256]{2,1,0:T(8,128)(2,1)}, bf16[2,512,256]{2,1,0:T(8,128)(2,1)}, u32[]{:S(2)}, u32[]{:S(2)}) collective-permute-start(bf16[2,512,256]{2,1,0:T(8,128)(2,1)} %collective-permute-done.15.refs_12_), channel_id=1, source_target_pairs={{32,56},{33,57},{34,58},{35,59},{36,60},{37,61},{38,62},{39,63},{4... | collective-permute-start | bytes 1572872 | tf_op jit(solution)/shard_map/ppermute | solution.py:85
  94.7 6.8 %copy-start.12 = (bf16[2,512,256]{2,1,0:T(8,128)(2,1)}, bf16[2,512,256]{2,1,0:T(8,128)(2,1)S(1)}, u32[]{:S(2)}) copy-start(bf16[2,512,256]{2,1,0:T(8,128)(2,1)S(1)} %collective-permute-done.20.refs_17_) | copy-start | bytes 1572868
  94.7 12.3 %collective-permute-start.21 = (bf16[2,512,256]{2,1,0:T(8,128)(2,1)}, bf16[2,512,256]{2,1,0:T(8,128)(2,1)}, u32[]{:S(2)}, u32[]{:S(2)}) collective-permute-start(bf16[2,512,256]{2,1,0:T(8,128)(2,1)} %collective-permute-done.13.refs_10_), channel_id=1, source_target_pairs={{0,7},{1,0},{2,1},{3,2},{4,3},{5,4},{6,5},{7,6},{8,15},{9,8},{10,9... | collective-permute-start | bytes 1572872 | tf_op jit(solution)/shard_map/ppermute | solution.py:85
  100.0 8.4 %collective-permute-start.18 = (bf16[2,512,256]{2,1,0:T(8,128)(2,1)}, bf16[2,512,256]{2,1,0:T(8,128)(2,1)}, u32[]{:S(2)}, u32[]{:S(2)}) collective-permute-start(bf16[2,512,256]{2,1,0:T(8,128)(2,1)} %collective-permute-done.12.refs_9_), channel_id=1, source_target_pairs={{0,1},{1,2},{2,3},{3,4},{4,5},{5,6},{6,7},{7,0},{8,9},{9,10},{10,1... | collective-permute-start | bytes 1572872 | tf_op jit(solution)/shard_map/ppermute | solution.py:85
  102.0 10.5 %collective-permute-start.17 = (bf16[2,512,256]{2,1,0:T(8,128)(2,1)}, bf16[2,512,256]{2,1,0:T(8,128)(2,1)}, u32[]{:S(2)}, u32[]{:S(2)}) collective-permute-start(bf16[2,512,256]{2,1,0:T(8,128)(2,1)} %collective-permute-done.11.refs_8_), channel_id=1, source_target_pairs={{0,1},{1,2},{2,3},{3,4},{4,5},{5,6},{6,7},{7,0},{8,9},{9,10},{10,1... | collective-permute-start | bytes 1572872 | tf_op jit(solution)/shard_map/ppermute | solution.py:85
  103.6 10.2 %collective-permute-start.24 = (bf16[2,512,256]{2,1,0:T(8,128)(2,1)}, bf16[2,512,256]{2,1,0:T(8,128)(2,1)}, u32[]{:S(2)}, u32[]{:S(2)}) collective-permute-start(bf16[2,512,256]{2,1,0:T(8,128)(2,1)} %collective-permute-done.16.refs_13_), channel_id=1, source_target_pairs={{32,56},{33,57},{34,58},{35,59},{36,60},{37,61},{38,62},{39,63},{4... | collective-permute-start | bytes 1572872 | tf_op jit(solution)/shard_map/ppermute | solution.py:85
  105.5 8.3 %collective-permute-start.22 = (bf16[2,512,256]{2,1,0:T(8,128)(2,1)}, bf16[2,512,256]{2,1,0:T(8,128)(2,1)}, u32[]{:S(2)}, u32[]{:S(2)}) collective-permute-start(bf16[2,512,256]{2,1,0:T(8,128)(2,1)} %collective-permute-done.14.refs_11_), channel_id=1, source_target_pairs={{0,7},{1,0},{2,1},{3,2},{4,3},{5,4},{6,5},{7,6},{8,15},{9,8},{10,9... | collective-permute-start | bytes 1572872 | tf_op jit(solution)/shard_map/ppermute | solution.py:85
  107.0 6.8 %collective-permute-start.25 = (bf16[2,512,256]{2,1,0:T(8,128)(2,1)}, bf16[2,512,256]{2,1,0:T(8,128)(2,1)}, u32[]{:S(2)}, u32[]{:S(2)}) collective-permute-start(bf16[2,512,256]{2,1,0:T(8,128)(2,1)} %collective-permute-done.21.refs_18_), channel_id=1, source_target_pairs={{0,7},{1,0},{2,1},{3,2},{4,3},{5,4},{6,5},{7,6},{8,15},{9,8},{10,9... | collective-permute-start | bytes 1572872 | tf_op jit(solution)/shard_map/ppermute | solution.py:85
  108.4 5.4 %collective-permute-start.26 = (bf16[2,512,256]{2,1,0:T(8,128)(2,1)}, bf16[2,512,256]{2,1,0:T(8,128)(2,1)}, u32[]{:S(2)}, u32[]{:S(2)}) collective-permute-start(bf16[2,512,256]{2,1,0:T(8,128)(2,1)} %collective-permute-done.18.refs_15_), channel_id=1, source_target_pairs={{0,1},{1,2},{2,3},{3,4},{4,5},{5,6},{6,7},{7,0},{8,9},{9,10},{10,1... | collective-permute-start | bytes 1572872 | tf_op jit(solution)/shard_map/ppermute | solution.py:85
  118.2 1.3 copy-start
  119.5 21.4 %all-to-all-start.1 = ((bf16[8,64,512]{2,1,0:T(8,128)(2,1)}), bf16[8,64,512]{2,1,0:T(8,128)(2,1)S(1)}, u32[]{:S(2)}, u32[]{:S(2)}) async-start(bf16[8,64,512]{2,1,0:T(8,128)(2,1)} %get-tuple-element.8), calls=%async_computation.1 | async-start | bytes 1048576 | tf_op jit(solution)/shard_map/all_to_all | solution.py:329
  162.5 3.6 %collective-permute-start.27 = (bf16[8,64,256]{2,1,0:T(8,128)(2,1)S(1)}, bf16[8,64,256]{2,1,0:T(8,128)(2,1)S(1)}, u32[]{:S(2)}, u32[]{:S(2)}) collective-permute-start(bf16[8,64,256]{2,1,0:T(8,128)(2,1)S(1)} %shard_map.62.own_ref), channel_id=1, source_target_pairs={{0,32},{32,0},{1,33},{33,1},{2,34},{34,2},{3,35},{35,3},{4,36},{36... | collective-permute-start | bytes 786440 | tf_op jit(solution)/shard_map/ppermute | solution.py:359
  167.5 52.2 %copy-start.1 = (bf16[8,512,256]{2,1,0:T(8,128)(2,1)S(1)}, bf16[8,512,256]{2,1,0:T(8,128)(2,1)}, u32[]{:S(2)}) copy-start(bf16[8,512,256]{2,1,0:T(8,128)(2,1)} %copy-done) | copy-start | bytes 6291460
  221.0 4.2 %collective-permute-start.28 = (bf16[8,64,128]{2,1,0:T(8,128)(2,1)S(1)}, bf16[8,64,128]{2,1,0:T(8,128)(2,1)S(1)}, u32[]{:S(2)}, u32[]{:S(2)}) collective-permute-start(bf16[8,64,128]{2,1,0:T(8,128)(2,1)S(1)} %get-tuple-element.13), channel_id=1, source_target_pairs={{0,32},{32,0},{1,33},{33,1},{2,34},{34,2},{3,35},{35,3},{4,36},{36... | collective-permute-start | bytes 393224 | tf_op jit(solution)/shard_map/ppermute | solution.py:374

commit v2 on v1

--- a/solution.py
+++ b/solution.py
@@ -43,7 +43,9 @@
     return hi, mid, low
 
 
-def slice_kernel(f_ref, cores_ref, o_ref, sem):
+def slice_kernel(f_ref, cores_hbm, o_ref, cores_ref, sem):
+    core = pltpu.make_async_copy(cores_hbm, cores_ref, sem.at[NZ])
+    core.start()
     copies = []
     for q in range(NZ):
         copies.append(
@@ -52,6 +54,7 @@
             )
         )
         copies[q].start()
+    core.wait()
     one, two, _ = split3(cores_ref[...])
     both = jnp.concatenate([one, two], axis=1)
     for q in range(NZ):
@@ -253,16 +256,22 @@
     work = jnp.concatenate([gram, unit], axis=1)
     blocks = [work[8 * b:8 * b + 8, :] for b in range(RANK // 8)]
     sub = lax.broadcasted_iota(jnp.int32, (8, 2 * RANK), 0)
-    for p in range(RANK):
+    for p in range(0, RANK, 2):
         home, at = divmod(p, 8)
-        row = blocks[home][at:at + 1, :]
-        pivot = row[:, p:p + 1]
-        scaled = row * (1.0 / pivot)
+        row0 = blocks[home][at:at + 1, :]
+        row1 = blocks[home][at + 1:at + 2, :]
+        top, side, low = row0[:, p:p + 1], row0[:, p + 1:p + 2], row1[:, p + 1:p + 2]
+        scale = 1.0 / (top * low - side * side)
+        first = (low * row0 - side * row1) * scale
+        second = (top * row1 - side * row0) * scale
+        inner = row1 - (side * (1.0 / top)) * row0
         for b in range(home, RANK // 8):
-            col = jnp.broadcast_to(blocks[b][:, p:p + 1], (8, 2 * RANK))
+            col0 = jnp.broadcast_to(blocks[b][:, p:p + 1], (8, 2 * RANK))
+            col1 = jnp.broadcast_to(blocks[b][:, p + 1:p + 2], (8, 2 * RANK))
+            new = blocks[b] - (col0 * first + col1 * second)
             if b == home:
-                col = jnp.where(sub > at, col, 0.0)
-            blocks[b] = blocks[b] - col * scaled
+                new = jnp.where(sub > at + 1, new, jnp.where(sub == at + 1, inner, blocks[b]))
+            blocks[b] = new
     work = jnp.concatenate(blocks, axis=0)
     diag = jnp.sum(jnp.where(row_id == col_id, work[:, 0:RANK], 0.0), axis=1, keepdims=True)
     return work[:, RANK:2 * RANK] * (1.0 / jnp.sqrt(diag))
@@ -306,7 +315,7 @@
     side = lax.axis_index("core").astype(jnp.int32).reshape(1)
     row_first = tile_list[:, 0].astype(jnp.int32)
     row_second = tile_list[:, 1].astype(jnp.int32)
-    params = pltpu.CompilerParams(vmem_limit_bytes=12 * 1024 * 1024)
+    params = pltpu.CompilerParams(vmem_limit_bytes=32 * 1024 * 1024)
 
     smem = pl.BlockSpec(memory_space=pltpu.SMEM)
     hbm = pl.BlockSpec(memory_space=pl.ANY)
@@ -332,10 +341,10 @@
     sliced = call(
         slice_kernel,
         shape(NZ, RANK, ROWS + 2 * RANK),
-        [hbm, vmem],
+        [hbm, hbm],
         in_hbm(mine),
-        cores[0],
-        scratch=[pltpu.SemaphoreType.DMA((NZ,))],
+        in_hbm(cores[0]),
+        scratch=[pltpu.VMEM((RANK, RANK), F32), pltpu.SemaphoreType.DMA((NZ + 1,))],
     )
     panels = exchange(sliced)
     pieces = panels[:, :, ROWS:ROWS + 2 * RANK].astype(F32)

time: 227 us -> 226 us (level)
  no operation moved by 1% of the time
where the time goes in v2:
time: 226 us; the launch traced here: 225 us
  blocking collectives  89.3 us (40%)
  starting transfers between devices  80.5 us (36%)
  waiting for transfers between devices  32.9 us (15%)
  Pallas kernels  15.6 us (7%)
  other arithmetic  4.14 us (2%)
    all_to_all x4, blocking collectives, exchange(): return lax.all_to_all(x, 'z', 0, 0, tiled=True)  89.3 us
    ppermute x20, starting transfers between devices, bundle_send(): return lax.ppermute(value, ('core', 'x', 'y'), pairs)  45.8 us
    ppermute x7, starting transfers between devices, send(): return lax.ppermute(value, ('core', 'x', 'y'), pairs)  25.5 us
    all_to_all x1, waiting for transfers between devices, exchange(): return lax.all_to_all(x, 'z', 0, 0, tiled=True)  17.8 us
    pallas_call x7, Pallas kernels, call(): pl.pallas_call(kernel, out_shape=out_shape, in_specs=in_specs, out_specs=...  15.6 us
    ppermute x20, waiting for transfers between devices, bundle_send(): return lax.ppermute(value, ('core', 'x', 'y'), pairs)  8.93 us
  transfers between devices with their start and end apart: 30, of which 10 were waited for; matrix products, arithmetic and copies ran while one was open for 2% of the time, Pallas kernels for 0%

profile of v2, /device:TPU:25, one launch (start us, length us, event | category | flops | bytes accessed | tf_op | source)
XLA Modules:
  0.0 225.0 jit_solution(15858147779631376769)
XLA Ops:
  1.6 23.4 %all_to_all.25 = bf16[8,64,384]{2,1,0:T(8,128)(2,1)S(1)} all-to-all(bf16[8,64,384]{2,1,0:T(8,128)(2,1)S(1)} %shard_map.59), channel_id=1, replica_groups=mesh['z'=8,'core'=2,'x'=4,'y'=8] {'z'}, dimensions={0} | all-to-all | bytes 786432 | tf_op jit(solution)/shard_map/all_to_all | solution.py:338
  25.0 4.4 %collective-permute-start = (bf16[512,256]{1,0:T(8,128)(2,1)S(1)}, bf16[512,256]{1,0:T(8,128)(2,1)S(1)}, u32[]{:S(2)}, u32[]{:S(2)}) collective-permute-start(bf16[512,256]{1,0:T(8,128)(2,1)S(1)} %bitcast.56), channel_id=1, source_target_pairs={{0,8},{32,33},{1,9},{33,34},{2,10},{34,35},{3,11},{35,36},{4,12},{... | collective-permute-start | bytes 786440 | tf_op jit(solution)/shard_map/ppermute | solution.py:78
  29.5 1.9 collective-permute-start.1
  31.4 1.4 collective-permute-done
  32.8 5.3 %collective-permute-start.2 = (bf16[512,256]{1,0:T(8,128)(2,1)S(1)}, bf16[512,256]{1,0:T(8,128)(2,1)S(1)}, u32[]{:S(2)}, u32[]{:S(2)}) collective-permute-start(bf16[512,256]{1,0:T(8,128)(2,1)S(1)} %collective-permute-done), channel_id=1, source_target_pairs={{0,8},{32,33},{1,9},{33,34},{2,10},{34,35},{3,11},{35,36},{4,12},{... | collective-permute-start | bytes 786440 | tf_op jit(solution)/shard_map/ppermute | solution.py:78
  38.1 1.9 collective-permute-start.3
  40.0 1.4 collective-permute-done.2
  41.4 5.0 %collective-permute-start.4 = (bf16[512,256]{1,0:T(8,128)(2,1)S(1)}, bf16[512,256]{1,0:T(8,128)(2,1)S(1)}, u32[]{:S(2)}, u32[]{:S(2)}) collective-permute-start(bf16[512,256]{1,0:T(8,128)(2,1)S(1)} %collective-permute-done.2), channel_id=1, source_target_pairs={{32,33},{33,34},{34,35},{35,36},{36,37},{37,38},{38,39},{39,32},{4... | collective-permute-start | bytes 786440 | tf_op jit(solution)/shard_map/ppermute | solution.py:78
  46.4 1.9 collective-permute-start.5
  48.3 1.4 collective-permute-done.4
  49.7 5.0 %collective-permute-start.6 = (bf16[512,256]{1,0:T(8,128)(2,1)S(1)}, bf16[512,256]{1,0:T(8,128)(2,1)S(1)}, u32[]{:S(2)}, u32[]{:S(2)}) collective-permute-start(bf16[512,256]{1,0:T(8,128)(2,1)S(1)} %collective-permute-done.4), channel_id=1, source_target_pairs={{32,33},{33,34},{34,35},{35,36},{36,37},{37,38},{38,39},{39,32},{4... | collective-permute-start | bytes 786440 | tf_op jit(solution)/shard_map/ppermute | solution.py:78
  54.8 4.1 %collective-permute-start.9 = (bf16[2,512,256]{2,1,0:T(8,128)(2,1)S(1)}, bf16[2,512,256]{2,1,0:T(8,128)(2,1)S(1)}, u32[]{:S(2)}, u32[]{:S(2)}) collective-permute-start(bf16[2,512,256]{2,1,0:T(8,128)(2,1)S(1)} %pad_maximum_fusion.refs_0_), channel_id=1, source_target_pairs={{0,7},{32,56},{1,0},{33,57},{2,1},{34,58},{3,2},{35,59},{4,3},{36,... | collective-permute-start | bytes 1572872 | tf_op jit(solution)/shard_map/ppermute | solution.py:88
  58.9 1.9 collective-permute-start.7
  60.9 4.6 %collective-permute-start.10 = (bf16[2,512,256]{2,1,0:T(8,128)(2,1)S(1)}, bf16[2,512,256]{2,1,0:T(8,128)(2,1)S(1)}, u32[]{:S(2)}, u32[]{:S(2)}) collective-permute-start(bf16[2,512,256]{2,1,0:T(8,128)(2,1)S(1)} %pad_maximum_fusion.1.refs_1_), channel_id=1, source_target_pairs={{0,7},{32,56},{1,0},{33,57},{2,1},{34,58},{3,2},{35,59},{4,3},{36,... | collective-permute-start | bytes 1572872 | tf_op jit(solution)/shard_map/ppermute | solution.py:88
  65.5 1.9 collective-permute-start.8
  67.5 1.9 collective-permute-start.19
  69.5 4.6 %collective-permute-start.15 = (bf16[2,512,256]{2,1,0:T(8,128)(2,1)S(1)}, bf16[2,512,256]{2,1,0:T(8,128)(2,1)}, u32[]{:S(2)}, u32[]{:S(2)}) collective-permute-start(bf16[2,512,256]{2,1,0:T(8,128)(2,1)S(1)} %pad_maximum_fusion.2.refs_2_), channel_id=1, source_target_pairs={{32,56},{33,57},{34,58},{35,59},{36,60},{37,61},{38,62},{39,63},{4... | collective-permute-start | bytes 1572872 | tf_op jit(solution)/shard_map/ppermute | solution.py:88
  74.1 1.5 collective-permute-start.13
  75.6 1.9 collective-permute-start.11
  77.5 2.8 %collective-permute-start.20 = (bf16[2,512,256]{2,1,0:T(8,128)(2,1)S(1)}, bf16[2,512,256]{2,1,0:T(8,128)(2,1)S(1)}, u32[]{:S(2)}, u32[]{:S(2)}) collective-permute-start(bf16[2,512,256]{2,1,0:T(8,128)(2,1)S(1)} %pad_maximum_fusion.3.refs_3_), channel_id=1, source_target_pairs={{32,40},{33,41},{34,42},{35,43},{36,44},{37,45},{38,46},{39,47},{4... | collective-permute-start | bytes 1572872 | tf_op jit(solution)/shard_map/ppermute | solution.py:88
  80.3 2.0 collective-permute-done.19.refs_16_
  82.3 1.9 collective-permute-start.12
  84.2 4.6 %collective-permute-start.16 = (bf16[2,512,256]{2,1,0:T(8,128)(2,1)S(1)}, bf16[2,512,256]{2,1,0:T(8,128)(2,1)}, u32[]{:S(2)}, u32[]{:S(2)}) collective-permute-start(bf16[2,512,256]{2,1,0:T(8,128)(2,1)S(1)} %pad_maximum_fusion.3.refs_3_), channel_id=1, source_target_pairs={{32,56},{33,57},{34,58},{35,59},{36,60},{37,61},{38,62},{39,63},{4... | collective-permute-start | bytes 1572872 | tf_op jit(solution)/shard_map/ppermute | solution.py:88
  88.8 1.5 collective-permute-start.14
  90.3 1.9 collective-permute-start.23
  92.2 1.7 collective-permute-done.20.refs_17_
  93.9 1.5 collective-permute-start.21
  95.4 3.8 %collective-permute-done.12.refs_9_ = bf16[2,512,256]{2,1,0:T(8,128)(2,1)} collective-permute-done((bf16[2,512,256]{2,1,0:T(8,128)(2,1)S(1)}, bf16[2,512,256]{2,1,0:T(8,128)(2,1)}, u32[]{:S(2)}, u32[]{:S(2)}) %collective-permute-start.12) | collective-permute-done | bytes 524320 | tf_op jit(solution)/shard_map/ppermute | solution.py:88
  99.3 1.5 collective-permute-start.18
  101.3 1.5 collective-permute-start.17
  102.8 1.9 collective-permute-start.24
  104.7 1.5 collective-permute-start.22
  106.2 1.5 collective-permute-start.25
  107.7 1.5 collective-permute-start.26
  111.7 1.4 collective-permute-done.24.refs_21_
  113.1 4.3 %shard_map.60 = (bf16[8,64,512]{2,1,0:T(8,128)(2,1)}, bf16[8,512,256]{2,1,0:T(8,128)(2,1)S(1)}, bf16[8,512,256]{2,1,0:T(8,128)(2,1)S(1)}) custom-call(s32[2,8]{1,0:T(2,128)S(1)} %pad_add_fusion.first_ref, s32[2,8]{1,0:T(2,128)S(1)} %pad_add_fusion.1.second_ref, s32[1]{0:T(128)} %bitcast.3.z_ref, bf16[8,64,2048]{2,1,0:T(8,128)(2,1)} %bitcast.55, ...), custom_call_target="tpu_custom_call" | custom-call | tf_op jit(solution)/shard_map/pallas_call | solution.py:325
  117.5 1.3 copy-done
  118.8 3.5 %all-to-all-start.1 = ((bf16[8,64,512]{2,1,0:T(8,128)(2,1)}), bf16[8,64,512]{2,1,0:T(8,128)(2,1)S(1)}, u32[]{:S(2)}, u32[]{:S(2)}) async-start(bf16[8,64,512]{2,1,0:T(8,128)(2,1)} %get-tuple-element.8), calls=%async_computation.1 | async-start | bytes 1048576 | tf_op jit(solution)/shard_map/all_to_all | solution.py:338
  122.5 17.8 %all-to-all-done.1.part_ref = bf16[8,64,512]{2,1,0:T(8,128)(2,1)S(1)} async-done(((bf16[8,64,512]{2,1,0:T(8,128)(2,1)}), bf16[8,64,512]{2,1,0:T(8,128)(2,1)S(1)}, u32[]{:S(2)}, u32[]{:S(2)}) %all-to-all-start.1) | async-done | bytes 524320 | tf_op jit(solution)/shard_map/all_to_all | solution.py:338
  140.9 20.3 %all_to_all.26.core_ref = bf16[8,64,512]{2,1,0:T(8,128)(2,1)S(1)} all-to-all(bf16[8,64,512]{2,1,0:T(8,128)(2,1)S(1)} %shard_map.61), channel_id=1, replica_groups=mesh['z'=8,'core'=2,'x'=4,'y'=8] {'z'}, dimensions={0} | all-to-all | bytes 1048576 | tf_op jit(solution)/shard_map/all_to_all | solution.py:338
  161.8 2.4 %collective-permute-start.27 = (bf16[8,64,256]{2,1,0:T(8,128)(2,1)S(1)}, bf16[8,64,256]{2,1,0:T(8,128)(2,1)S(1)}, u32[]{:S(2)}, u32[]{:S(2)}) collective-permute-start(bf16[8,64,256]{2,1,0:T(8,128)(2,1)S(1)} %shard_map.62.own_ref), channel_id=1, source_target_pairs={{0,32},{32,0},{1,33},{33,1},{2,34},{34,2},{3,35},{35,3},{4,36},{36... | collective-permute-start | bytes 786440 | tf_op jit(solution)/shard_map/ppermute | solution.py:368
  164.2 1.1 collective-permute-done.27.other_ref
  165.3 1.4 shard_map.63
  166.8 23.3 %all_to_all.27.part_ref = bf16[8,80,512]{2,1,0:T(8,128)(2,1)S(1)} all-to-all(bf16[8,80,512]{2,1,0:T(8,128)(2,1)S(1)} %shard_map.63), channel_id=1, replica_groups=mesh['z'=8,'core'=2,'x'=4,'y'=8] {'z'}, dimensions={0} | all-to-all | bytes 1310720 | tf_op jit(solution)/shard_map/all_to_all | solution.py:338
  190.0 6.3 %shard_map.64 = bf16[8,80,512]{2,1,0:T(8,128)(2,1)S(1)} custom-call(bf16[8,80,512]{2,1,0:T(8,128)(2,1)S(1)} %all_to_all.27.part_ref, f32[8,64,64]{2,1,0:T(8,128)S(1)} %slice_add_fusion.cores_ref), custom_call_target="tpu_custom_call" | custom-call | tf_op jit(solution)/shard_map/pallas_call | solution.py:325
  196.4 22.3 %all_to_all.28.core_ref = bf16[8,80,512]{2,1,0:T(8,128)(2,1)S(1)} all-to-all(bf16[8,80,512]{2,1,0:T(8,128)(2,1)S(1)} %shard_map.64), channel_id=1, replica_groups=mesh['z'=8,'core'=2,'x'=4,'y'=8] {'z'}, dimensions={0} | all-to-all | bytes 1310720 | tf_op jit(solution)/shard_map/all_to_all | solution.py:338
  218.6 1.4 shard_map.65
  220.0 3.3 %collective-permute-start.28 = (bf16[8,64,128]{2,1,0:T(8,128)(2,1)S(1)}, bf16[8,64,128]{2,1,0:T(8,128)(2,1)S(1)}, u32[]{:S(2)}, u32[]{:S(2)}) collective-permute-start(bf16[8,64,128]{2,1,0:T(8,128)(2,1)S(1)} %get-tuple-element.13), channel_id=1, source_target_pairs={{0,32},{32,0},{1,33},{33,1},{2,34},{34,2},{3,35},{35,3},{4,36},{36... | collective-permute-start | bytes 393224 | tf_op jit(solution)/shard_map/ppermute | solution.py:383
  (62 shorter events, 7.4 us)
Async XLA Ops:
  25.0 7.7 %collective-permute-start = (bf16[512,256]{1,0:T(8,128)(2,1)S(1)}, bf16[512,256]{1,0:T(8,128)(2,1)S(1)}, u32[]{:S(2)}, u32[]{:S(2)}) collective-permute-start(bf16[512,256]{1,0:T(8,128)(2,1)S(1)} %bitcast.56), channel_id=1, source_target_pairs={{0,8},{32,33},{1,9},{33,34},{2,10},{34,35},{3,11},{35,36},{4,12},{... | collective-permute-start | bytes 786440 | tf_op jit(solution)/shard_map/ppermute | solution.py:78
  29.5 8.6 %collective-permute-start.1 = (bf16[512,256]{1,0:T(8,128)(2,1)S(1)}, bf16[512,256]{1,0:T(8,128)(2,1)S(1)}, u32[]{:S(2)}, u32[]{:S(2)}) collective-permute-start(bf16[512,256]{1,0:T(8,128)(2,1)S(1)} %bitcast.57), channel_id=1, source_target_pairs={{0,24},{32,39},{1,25},{33,32},{2,26},{34,33},{3,27},{35,34},{4,28}... | collective-permute-start | bytes 786440 | tf_op jit(solution)/shard_map/ppermute | solution.py:78
  32.8 8.6 %collective-permute-start.2 = (bf16[512,256]{1,0:T(8,128)(2,1)S(1)}, bf16[512,256]{1,0:T(8,128)(2,1)S(1)}, u32[]{:S(2)}, u32[]{:S(2)}) collective-permute-start(bf16[512,256]{1,0:T(8,128)(2,1)S(1)} %collective-permute-done), channel_id=1, source_target_pairs={{0,8},{32,33},{1,9},{33,34},{2,10},{34,35},{3,11},{35,36},{4,12},{... | collective-permute-start | bytes 786440 | tf_op jit(solution)/shard_map/ppermute | solution.py:78
  38.1 8.3 %collective-permute-start.3 = (bf16[512,256]{1,0:T(8,128)(2,1)S(1)}, bf16[512,256]{1,0:T(8,128)(2,1)S(1)}, u32[]{:S(2)}, u32[]{:S(2)}) collective-permute-start(bf16[512,256]{1,0:T(8,128)(2,1)S(1)} %collective-permute-done.1), channel_id=1, source_target_pairs={{32,39},{33,32},{34,33},{35,34},{36,35},{37,36},{38,37},{39,38},{4... | collective-permute-start | bytes 786440 | tf_op jit(solution)/shard_map/ppermute | solution.py:78
  41.4 8.3 %collective-permute-start.4 = (bf16[512,256]{1,0:T(8,128)(2,1)S(1)}, bf16[512,256]{1,0:T(8,128)(2,1)S(1)}, u32[]{:S(2)}, u32[]{:S(2)}) collective-permute-start(bf16[512,256]{1,0:T(8,128)(2,1)S(1)} %collective-permute-done.2), channel_id=1, source_target_pairs={{32,33},{33,34},{34,35},{35,36},{36,37},{37,38},{38,39},{39,32},{4... | collective-permute-start | bytes 786440 | tf_op jit(solution)/shard_map/ppermute | solution.py:78
  46.4 19.1 %collective-permute-start.5 = (bf16[512,256]{1,0:T(8,128)(2,1)S(1)}, bf16[512,256]{1,0:T(8,128)(2,1)S(1)}, u32[]{:S(2)}, u32[]{:S(2)}) collective-permute-start(bf16[512,256]{1,0:T(8,128)(2,1)S(1)} %collective-permute-done.3), channel_id=1, source_target_pairs={{32,39},{33,32},{34,33},{35,34},{36,35},{37,36},{38,37},{39,38},{4... | collective-permute-start | bytes 786440 | tf_op jit(solution)/shard_map/ppermute | solution.py:78
  49.7 17.8 %collective-permute-start.6 = (bf16[512,256]{1,0:T(8,128)(2,1)S(1)}, bf16[512,256]{1,0:T(8,128)(2,1)S(1)}, u32[]{:S(2)}, u32[]{:S(2)}) collective-permute-start(bf16[512,256]{1,0:T(8,128)(2,1)S(1)} %collective-permute-done.4), channel_id=1, source_target_pairs={{32,33},{33,34},{34,35},{35,36},{36,37},{37,38},{38,39},{39,32},{4... | collective-permute-start | bytes 786440 | tf_op jit(solution)/shard_map/ppermute | solution.py:78
  54.7 46.0 %copy-start.12 = (s32[8,2]{0,1:T(2,128)S(1)}, s32[8,2]{0,1:T(2,128)}, u32[]{:S(2)}) copy-start(s32[8,2]{0,1:T(2,128)} %param.6) | copy-start | bytes 196
  54.8 58.3 %copy-start.2 = (bf16[2,512,256]{2,1,0:T(8,128)(2,1)}, bf16[2,512,256]{2,1,0:T(8,128)(2,1)S(1)}, u32[]{:S(2)}) copy-start(bf16[2,512,256]{2,1,0:T(8,128)(2,1)S(1)} %pad_maximum_fusion.refs_0_) | copy-start | bytes 1572868
  54.8 14.7 %collective-permute-start.9 = (bf16[2,512,256]{2,1,0:T(8,128)(2,1)S(1)}, bf16[2,512,256]{2,1,0:T(8,128)(2,1)S(1)}, u32[]{:S(2)}, u32[]{:S(2)}) collective-permute-start(bf16[2,512,256]{2,1,0:T(8,128)(2,1)S(1)} %pad_maximum_fusion.refs_0_), channel_id=1, source_target_pairs={{0,7},{32,56},{1,0},{33,57},{2,1},{34,58},{3,2},{35,59},{4,3},{36,... | collective-permute-start | bytes 1572872 | tf_op jit(solution)/shard_map/ppermute | solution.py:88
  58.9 15.2 %collective-permute-start.7 = (bf16[2,512,256]{2,1,0:T(8,128)(2,1)S(1)}, bf16[2,512,256]{2,1,0:T(8,128)(2,1)S(1)}, u32[]{:S(2)}, u32[]{:S(2)}) collective-permute-start(bf16[2,512,256]{2,1,0:T(8,128)(2,1)S(1)} %pad_maximum_fusion.refs_0_), channel_id=1, source_target_pairs={{0,1},{32,40},{1,2},{33,41},{2,3},{34,42},{3,4},{35,43},{4,5},{36,... | collective-permute-start | bytes 1572872 | tf_op jit(solution)/shard_map/ppermute | solution.py:88
  60.9 52.2 %copy-start.3 = (bf16[2,512,256]{2,1,0:T(8,128)(2,1)}, bf16[2,512,256]{2,1,0:T(8,128)(2,1)S(1)}, u32[]{:S(2)}) copy-start(bf16[2,512,256]{2,1,0:T(8,128)(2,1)S(1)} %pad_maximum_fusion.1.refs_1_) | copy-start | bytes 1572868
  60.9 14.7 %collective-permute-start.10 = (bf16[2,512,256]{2,1,0:T(8,128)(2,1)S(1)}, bf16[2,512,256]{2,1,0:T(8,128)(2,1)S(1)}, u32[]{:S(2)}, u32[]{:S(2)}) collective-permute-start(bf16[2,512,256]{2,1,0:T(8,128)(2,1)S(1)} %pad_maximum_fusion.1.refs_1_), channel_id=1, source_target_pairs={{0,7},{32,56},{1,0},{33,57},{2,1},{34,58},{3,2},{35,59},{4,3},{36,... | collective-permute-start | bytes 1572872 | tf_op jit(solution)/shard_map/ppermute | solution.py:88
  65.5 12.0 %copy-start.4 = (bf16[2,512,256]{2,1,0:T(8,128)(2,1)}, bf16[2,512,256]{2,1,0:T(8,128)(2,1)S(1)}, u32[]{:S(2)}) copy-start(bf16[2,512,256]{2,1,0:T(8,128)(2,1)S(1)} %pad_maximum_fusion.2.refs_2_) | copy-start | bytes 1572868
  65.5 12.0 %collective-permute-start.8 = (bf16[2,512,256]{2,1,0:T(8,128)(2,1)S(1)}, bf16[2,512,256]{2,1,0:T(8,128)(2,1)S(1)}, u32[]{:S(2)}, u32[]{:S(2)}) collective-permute-start(bf16[2,512,256]{2,1,0:T(8,128)(2,1)S(1)} %pad_maximum_fusion.1.refs_1_), channel_id=1, source_target_pairs={{0,1},{32,40},{1,2},{33,41},{2,3},{34,42},{3,4},{35,43},{4,5},{36,... | collective-permute-start | bytes 1572872 | tf_op jit(solution)/shard_map/ppermute | solution.py:88
  67.5 14.8 %collective-permute-start.19 = (bf16[2,512,256]{2,1,0:T(8,128)(2,1)S(1)}, bf16[2,512,256]{2,1,0:T(8,128)(2,1)S(1)}, u32[]{:S(2)}, u32[]{:S(2)}) collective-permute-start(bf16[2,512,256]{2,1,0:T(8,128)(2,1)S(1)} %pad_maximum_fusion.2.refs_2_), channel_id=1, source_target_pairs={{32,40},{33,41},{34,42},{35,43},{36,44},{37,45},{38,46},{39,47},{4... | collective-permute-start | bytes 1572872 | tf_op jit(solution)/shard_map/ppermute | solution.py:88
  69.5 43.6 %copy-start.5 = (bf16[2,512,256]{2,1,0:T(8,128)(2,1)}, bf16[2,512,256]{2,1,0:T(8,128)(2,1)S(1)}, u32[]{:S(2)}) copy-start(bf16[2,512,256]{2,1,0:T(8,128)(2,1)S(1)} %pad_maximum_fusion.3.refs_3_) | copy-start | bytes 1572868
  69.5 43.6 %copy-start.6 = (bf16[2,512,256]{2,1,0:T(8,128)(2,1)}, bf16[2,512,256]{2,1,0:T(8,128)(2,1)S(1)}, u32[]{:S(2)}) copy-start(bf16[2,512,256]{2,1,0:T(8,128)(2,1)S(1)} %collective-permute-done.9.refs_6_) | copy-start | bytes 1572868
  69.5 14.7 %collective-permute-start.15 = (bf16[2,512,256]{2,1,0:T(8,128)(2,1)S(1)}, bf16[2,512,256]{2,1,0:T(8,128)(2,1)}, u32[]{:S(2)}, u32[]{:S(2)}) collective-permute-start(bf16[2,512,256]{2,1,0:T(8,128)(2,1)S(1)} %pad_maximum_fusion.2.refs_2_), channel_id=1, source_target_pairs={{32,56},{33,57},{34,58},{35,59},{36,60},{37,61},{38,62},{39,63},{4... | collective-permute-start | bytes 1572872 | tf_op jit(solution)/shard_map/ppermute | solution.py:88
  74.1 39.0 %copy-start.7 = (bf16[2,512,256]{2,1,0:T(8,128)(2,1)}, bf16[2,512,256]{2,1,0:T(8,128)(2,1)S(1)}, u32[]{:S(2)}) copy-start(bf16[2,512,256]{2,1,0:T(8,128)(2,1)S(1)} %collective-permute-done.7.refs_4_) | copy-start | bytes 1572868
  74.1 14.7 %collective-permute-start.13 = (bf16[2,512,256]{2,1,0:T(8,128)(2,1)S(1)}, bf16[2,512,256]{2,1,0:T(8,128)(2,1)}, u32[]{:S(2)}, u32[]{:S(2)}) collective-permute-start(bf16[2,512,256]{2,1,0:T(8,128)(2,1)S(1)} %collective-permute-done.9.refs_6_), channel_id=1, source_target_pairs={{0,7},{1,0},{2,1},{3,2},{4,3},{5,4},{6,5},{7,6},{8,15},{9,8},{10,9... | collective-permute-start | bytes 1572872 | tf_op jit(solution)/shard_map/ppermute | solution.py:88
  75.6 37.5 %copy-start.8 = (bf16[2,512,256]{2,1,0:T(8,128)(2,1)}, bf16[2,512,256]{2,1,0:T(8,128)(2,1)S(1)}, u32[]{:S(2)}) copy-start(bf16[2,512,256]{2,1,0:T(8,128)(2,1)S(1)} %collective-permute-done.10.refs_7_) | copy-start | bytes 1572868
  75.6 14.7 %collective-permute-start.11 = (bf16[2,512,256]{2,1,0:T(8,128)(2,1)S(1)}, bf16[2,512,256]{2,1,0:T(8,128)(2,1)}, u32[]{:S(2)}, u32[]{:S(2)}) collective-permute-start(bf16[2,512,256]{2,1,0:T(8,128)(2,1)S(1)} %collective-permute-done.7.refs_4_), channel_id=1, source_target_pairs={{0,1},{32,40},{1,2},{33,41},{2,3},{34,42},{3,4},{35,43},{4,5},{36,... | collective-permute-start | bytes 1572872 | tf_op jit(solution)/shard_map/ppermute | solution.py:88
  77.5 16.4 %copy-start.9 = (bf16[2,512,256]{2,1,0:T(8,128)(2,1)}, bf16[2,512,256]{2,1,0:T(8,128)(2,1)S(1)}, u32[]{:S(2)}) copy-start(bf16[2,512,256]{2,1,0:T(8,128)(2,1)S(1)} %collective-permute-done.8.refs_5_) | copy-start | bytes 1572868
  77.5 16.4 %collective-permute-start.20 = (bf16[2,512,256]{2,1,0:T(8,128)(2,1)S(1)}, bf16[2,512,256]{2,1,0:T(8,128)(2,1)S(1)}, u32[]{:S(2)}, u32[]{:S(2)}) collective-permute-start(bf16[2,512,256]{2,1,0:T(8,128)(2,1)S(1)} %pad_maximum_fusion.3.refs_3_), channel_id=1, source_target_pairs={{32,40},{33,41},{34,42},{35,43},{36,44},{37,45},{38,46},{39,47},{4... | collective-permute-start | bytes 1572872 | tf_op jit(solution)/shard_map/ppermute | solution.py:88
  82.3 17.0 %copy-start.10 = (bf16[2,512,256]{2,1,0:T(8,128)(2,1)}, bf16[2,512,256]{2,1,0:T(8,128)(2,1)S(1)}, u32[]{:S(2)}) copy-start(bf16[2,512,256]{2,1,0:T(8,128)(2,1)S(1)} %collective-permute-done.19.refs_16_) | copy-start | bytes 1572868
  82.3 17.0 %collective-permute-start.12 = (bf16[2,512,256]{2,1,0:T(8,128)(2,1)S(1)}, bf16[2,512,256]{2,1,0:T(8,128)(2,1)}, u32[]{:S(2)}, u32[]{:S(2)}) collective-permute-start(bf16[2,512,256]{2,1,0:T(8,128)(2,1)S(1)} %collective-permute-done.8.refs_5_), channel_id=1, source_target_pairs={{0,1},{32,40},{1,2},{33,41},{2,3},{34,42},{3,4},{35,43},{4,5},{36,... | collective-permute-start | bytes 1572872 | tf_op jit(solution)/shard_map/ppermute | solution.py:88
  84.2 17.1 %collective-permute-start.16 = (bf16[2,512,256]{2,1,0:T(8,128)(2,1)S(1)}, bf16[2,512,256]{2,1,0:T(8,128)(2,1)}, u32[]{:S(2)}, u32[]{:S(2)}) collective-permute-start(bf16[2,512,256]{2,1,0:T(8,128)(2,1)S(1)} %pad_maximum_fusion.3.refs_3_), channel_id=1, source_target_pairs={{32,56},{33,57},{34,58},{35,59},{36,60},{37,61},{38,62},{39,63},{4... | collective-permute-start | bytes 1572872 | tf_op jit(solution)/shard_map/ppermute | solution.py:88
  88.8 14.0 %collective-permute-start.14 = (bf16[2,512,256]{2,1,0:T(8,128)(2,1)S(1)}, bf16[2,512,256]{2,1,0:T(8,128)(2,1)}, u32[]{:S(2)}, u32[]{:S(2)}) collective-permute-start(bf16[2,512,256]{2,1,0:T(8,128)(2,1)S(1)} %collective-permute-done.10.refs_7_), channel_id=1, source_target_pairs={{0,7},{1,0},{2,1},{3,2},{4,3},{5,4},{6,5},{7,6},{8,15},{9,8},{10,9... | collective-permute-start | bytes 1572872 | tf_op jit(solution)/shard_map/ppermute | solution.py:88
  90.3 14.4 %collective-permute-start.23 = (bf16[2,512,256]{2,1,0:T(8,128)(2,1)}, bf16[2,512,256]{2,1,0:T(8,128)(2,1)}, u32[]{:S(2)}, u32[]{:S(2)}) collective-permute-start(bf16[2,512,256]{2,1,0:T(8,128)(2,1)} %collective-permute-done.15.refs_12_), channel_id=1, source_target_pairs={{32,56},{33,57},{34,58},{35,59},{36,60},{37,61},{38,62},{39,63},{4... | collective-permute-start | bytes 1572872 | tf_op jit(solution)/shard_map/ppermute | solution.py:88
  93.9 6.8 %copy-start.11 = (bf16[2,512,256]{2,1,0:T(8,128)(2,1)}, bf16[2,512,256]{2,1,0:T(8,128)(2,1)S(1)}, u32[]{:S(2)}) copy-start(bf16[2,512,256]{2,1,0:T(8,128)(2,1)S(1)} %collective-permute-done.20.refs_17_) | copy-start | bytes 1572868
  93.9 12.3 %collective-permute-start.21 = (bf16[2,512,256]{2,1,0:T(8,128)(2,1)}, bf16[2,512,256]{2,1,0:T(8,128)(2,1)}, u32[]{:S(2)}, u32[]{:S(2)}) collective-permute-start(bf16[2,512,256]{2,1,0:T(8,128)(2,1)} %collective-permute-done.13.refs_10_), channel_id=1, source_target_pairs={{0,7},{1,0},{2,1},{3,2},{4,3},{5,4},{6,5},{7,6},{8,15},{9,8},{10,9... | collective-permute-start | bytes 1572872 | tf_op jit(solution)/shard_map/ppermute | solution.py:88
  99.3 8.4 %collective-permute-start.18 = (bf16[2,512,256]{2,1,0:T(8,128)(2,1)}, bf16[2,512,256]{2,1,0:T(8,128)(2,1)}, u32[]{:S(2)}, u32[]{:S(2)}) collective-permute-start(bf16[2,512,256]{2,1,0:T(8,128)(2,1)} %collective-permute-done.12.refs_9_), channel_id=1, source_target_pairs={{0,1},{1,2},{2,3},{3,4},{4,5},{5,6},{6,7},{7,0},{8,9},{9,10},{10,1... | collective-permute-start | bytes 1572872 | tf_op jit(solution)/shard_map/ppermute | solution.py:88
  101.3 10.4 %collective-permute-start.17 = (bf16[2,512,256]{2,1,0:T(8,128)(2,1)}, bf16[2,512,256]{2,1,0:T(8,128)(2,1)}, u32[]{:S(2)}, u32[]{:S(2)}) collective-permute-start(bf16[2,512,256]{2,1,0:T(8,128)(2,1)} %collective-permute-done.11.refs_8_), channel_id=1, source_target_pairs={{0,1},{1,2},{2,3},{3,4},{4,5},{5,6},{6,7},{7,0},{8,9},{9,10},{10,1... | collective-permute-start | bytes 1572872 | tf_op jit(solution)/shard_map/ppermute | solution.py:88
  102.8 10.2 %collective-permute-start.24 = (bf16[2,512,256]{2,1,0:T(8,128)(2,1)}, bf16[2,512,256]{2,1,0:T(8,128)(2,1)}, u32[]{:S(2)}, u32[]{:S(2)}) collective-permute-start(bf16[2,512,256]{2,1,0:T(8,128)(2,1)} %collective-permute-done.16.refs_13_), channel_id=1, source_target_pairs={{32,56},{33,57},{34,58},{35,59},{36,60},{37,61},{38,62},{39,63},{4... | collective-permute-start | bytes 1572872 | tf_op jit(solution)/shard_map/ppermute | solution.py:88
  104.7 8.3 %collective-permute-start.22 = (bf16[2,512,256]{2,1,0:T(8,128)(2,1)}, bf16[2,512,256]{2,1,0:T(8,128)(2,1)}, u32[]{:S(2)}, u32[]{:S(2)}) collective-permute-start(bf16[2,512,256]{2,1,0:T(8,128)(2,1)} %collective-permute-done.14.refs_11_), channel_id=1, source_target_pairs={{0,7},{1,0},{2,1},{3,2},{4,3},{5,4},{6,5},{7,6},{8,15},{9,8},{10,9... | collective-permute-start | bytes 1572872 | tf_op jit(solution)/shard_map/ppermute | solution.py:88
  106.2 6.8 %collective-permute-start.25 = (bf16[2,512,256]{2,1,0:T(8,128)(2,1)}, bf16[2,512,256]{2,1,0:T(8,128)(2,1)}, u32[]{:S(2)}, u32[]{:S(2)}) collective-permute-start(bf16[2,512,256]{2,1,0:T(8,128)(2,1)} %collective-permute-done.21.refs_18_), channel_id=1, source_target_pairs={{0,7},{1,0},{2,1},{3,2},{4,3},{5,4},{6,5},{7,6},{8,15},{9,8},{10,9... | collective-permute-start | bytes 1572872 | tf_op jit(solution)/shard_map/ppermute | solution.py:88
  107.7 5.4 %collective-permute-start.26 = (bf16[2,512,256]{2,1,0:T(8,128)(2,1)}, bf16[2,512,256]{2,1,0:T(8,128)(2,1)}, u32[]{:S(2)}, u32[]{:S(2)}) collective-permute-start(bf16[2,512,256]{2,1,0:T(8,128)(2,1)} %collective-permute-done.18.refs_15_), channel_id=1, source_target_pairs={{0,1},{1,2},{2,3},{3,4},{4,5},{5,6},{6,7},{7,0},{8,9},{9,10},{10,1... | collective-permute-start | bytes 1572872 | tf_op jit(solution)/shard_map/ppermute | solution.py:88
  117.5 1.3 copy-start
  118.8 21.5 %all-to-all-start.1 = ((bf16[8,64,512]{2,1,0:T(8,128)(2,1)}), bf16[8,64,512]{2,1,0:T(8,128)(2,1)S(1)}, u32[]{:S(2)}, u32[]{:S(2)}) async-start(bf16[8,64,512]{2,1,0:T(8,128)(2,1)} %get-tuple-element.8), calls=%async_computation.1 | async-start | bytes 1048576 | tf_op jit(solution)/shard_map/all_to_all | solution.py:338
  161.8 3.6 %collective-permute-start.27 = (bf16[8,64,256]{2,1,0:T(8,128)(2,1)S(1)}, bf16[8,64,256]{2,1,0:T(8,128)(2,1)S(1)}, u32[]{:S(2)}, u32[]{:S(2)}) collective-permute-start(bf16[8,64,256]{2,1,0:T(8,128)(2,1)S(1)} %shard_map.62.own_ref), channel_id=1, source_target_pairs={{0,32},{32,0},{1,33},{33,1},{2,34},{34,2},{3,35},{35,3},{4,36},{36... | collective-permute-start | bytes 786440 | tf_op jit(solution)/shard_map/ppermute | solution.py:368
  166.8 51.9 %copy-start.1 = (bf16[8,512,256]{2,1,0:T(8,128)(2,1)S(1)}, bf16[8,512,256]{2,1,0:T(8,128)(2,1)}, u32[]{:S(2)}) copy-start(bf16[8,512,256]{2,1,0:T(8,128)(2,1)} %copy-done) | copy-start | bytes 6291460
  220.0 4.3 %collective-permute-start.28 = (bf16[8,64,128]{2,1,0:T(8,128)(2,1)S(1)}, bf16[8,64,128]{2,1,0:T(8,128)(2,1)S(1)}, u32[]{:S(2)}, u32[]{:S(2)}) collective-permute-start(bf16[8,64,128]{2,1,0:T(8,128)(2,1)S(1)} %get-tuple-element.13), channel_id=1, source_target_pairs={{0,32},{32,0},{1,33},{33,1},{2,34},{34,2},{3,35},{35,3},{4,36},{36... | collective-permute-start | bytes 393224 | tf_op jit(solution)/shard_map/ppermute | solution.py:383
